TPU v7x, 256 devices: a whole 4x4x8 slice. The times are simulated.
256 devices in a mesh: tm: 4 (over y), space: 64 (over x, z, core).
Axes of the slice: x: 4, y: 4, z: 8, core: 2. Of those that a mesh axis runs over, the one named last changes fastest.
Arguments:
- queries: bfloat16 [16, 4096, 1536], P('tm', 'space'), may hold values from -48 to 48
- key_rows: bfloat16 [16, 4096, 1536], P('tm', 'space'), may hold values from -4 to 4
- value_rows: bfloat16 [16, 4096, 1536], P('tm', 'space'), may hold values from -6 to 6
- dropout: int32 [4, 16, 4096, 12], P(None, 'tm', 'space'), may hold values 0 or 1
- tile_lists: int32 [64, 2], P('space'), may hold values from 0 to 63, as said below
Outputs:
- sampled_heads: bfloat16 [4, 16, 4096, 1536], P(None, 'tm', 'space')
Inputs may be any that keep to these rules, and one draw needn't show every extreme that they name: `tile_lists`: row t holds t first and then (t - 1) or (t + 1) modulo 64.
All inputs are finite; a program needn't handle non-finite values. No bound on the sum of `dropout` on one device may be relied on, other than what follows from the above.
Results may differ from a plain program's by a relative error of at most 0.0045.
Values may be sent and summed in bfloat16 or wider, within the bound.
No kernel may reach another device: no remote copies, remote signals or barrier semaphores. Data moves between devices by JAX's collectives and lax.ppermute only.
A program may use at most 128 MiB of HBM per device.

v0:
```python
import functools
import math

import jax
import jax.numpy as jnp
from jax import lax
from jax.experimental import pallas as pl
from jax.experimental.pallas import tpu as pltpu
from jax.sharding import PartitionSpec as P

keep_rate = 0.9

F32 = jnp.float32
BF16 = jnp.bfloat16
ANY = pl.BlockSpec(memory_space=pl.ANY)
HBM = pl.BlockSpec(memory_space=pltpu.HBM)
BITS = 16
LIMIT = 12 << 20
PACK_LIMIT = 60 << 20


def paired(x, axis, mate):
    return lax.ppermute(x, axis, [(i, mate(i)) for i in range(lax.axis_size(axis))])


def layout(package, rows):
    at = 2 * rows + BITS
    return at + rows * len(package[1])


def pack_body(q, k, v, drop, *refs, peers, per_dev, packages, rows, dim):
    outs = refs[: peers * len(packages)]
    in_sem = refs[-1]
    me = lax.axis_index("tm")
    zero = jnp.zeros((BITS, dim - drop.shape[3]), BF16)
    plan = [(n, i) for n in range(len(packages)) for i in tuple(range(1, peers)) + (0,)]
    loads = []
    for n, i in plan:
        chunk, asked = packages[n]
        out = outs[n * peers + i]
        parts = [(k, chunk, 0), (v, chunk, rows)]
        parts += [(q, c, (2 + m) * rows + BITS) for m, c in enumerate(asked)]
        for m, (x, c, at) in enumerate(parts):
            where = pl.ds(pl.multiple_of(((me ^ i) * per_dev + c) * dim, dim), dim)
            loads.append(
                pltpu.make_async_copy(x.at[:, where], out.at[pl.ds(at, rows)], in_sem.at[n, i, m])
            )
            loads[-1].start()
    for n, i in plan:
        bits = drop[:, (me ^ i) * per_dev + packages[n][0]].reshape(BITS, drop.shape[3])
        outs[n * peers + i][2 * rows : 2 * rows + BITS, :] = jnp.concatenate(
            [bits.astype(F32).astype(BF16), zero], axis=1
        )
    for copy in loads:
        copy.wait()


def pack(q, k, v, drop, per_dev, peers, packages):
    rows, width = q.shape
    dim = width // (per_dev * peers)
    sizes = [layout(package, rows) for package in packages for _ in range(peers)]
    flat = pl.pallas_call(
        functools.partial(
            pack_body, peers=peers, per_dev=per_dev, packages=packages, rows=rows, dim=dim
        ),
        in_specs=[HBM, HBM, HBM, pl.BlockSpec(memory_space=pltpu.VMEM)],
        out_specs=[pl.BlockSpec(memory_space=pltpu.VMEM)] * len(sizes),
        scratch_shapes=[
            pltpu.SemaphoreType.DMA((len(packages), peers, 2 + max(len(p[1]) for p in packages)))
        ],
        out_shape=[pltpu.VMEM((size, dim), BF16) for size in sizes],
        compiler_params=pltpu.CompilerParams(vmem_limit_bytes=PACK_LIMIT),
        cost_estimate=pl.CostEstimate(
            flops=0, bytes_accessed=4 * sum(sizes) * dim, transcendentals=0
        ),
        name="pack",
    )(q, k, v, drop)
    return [flat[n * peers : (n + 1) * peers] for n in range(len(packages))]


def attend_body(
    lists, column, near, far, *refs, slots, ask_at, rows, tok, samples, factor
):
    asks = refs[:slots]
    outs = refs[slots : 2 * slots]
    keys, vals, q_buf, done, out_sem = refs[2 * slots :]
    dim = near.shape[2]
    half = rows // 2
    span_keys = 2 * rows
    me = lax.axis_index("tm")
    use_near = lists[0, 1] == (lax.axis_index("space") ^ 1)

    for i in range(slots):
        q_buf[me ^ i] = asks[i][ask_at : ask_at + rows, :]

    def part(s, side, at, size):
        slot = me ^ s
        if side == 0:
            return column[slot, at : at + size, :]
        return jnp.where(use_near, near[slot, at : at + size, :], far[slot, at : at + size, :])

    def stage_keys(s):
        for late in range(2):
            for side in range(2):
                at = s * span_keys + (2 * late + side) * half
                keys[at : at + half, :] = part(s, side, late * half, half)

    def stage_values(s):
        for side in range(2):
            turned = part(s, side, 2 * rows, BITS).T
            for f in range(rows // tok):
                value = part(s, side, rows + f * tok, tok)
                late, rest = divmod(f * tok, half)
                at = s * span_keys + (2 * late + side) * half + rest
                for n in range(samples):
                    r = n * (rows // tok) + f
                    keep = jnp.broadcast_to(turned[0:tok, r : r + 1], (tok, dim))
                    vals[at : at + tok, n * dim : (n + 1) * dim] = value * keep

    row_frame = lax.broadcasted_iota(jnp.int32, (rows, rows), 0) // tok
    key_frame = lax.rem(lax.broadcasted_iota(jnp.int32, (rows, rows), 1), half) // tok
    early = key_frame <= row_frame
    late = (key_frame <= row_frame)[:half]
    scale = factor * math.log2(math.e)

    def dot_keys(q, lo, hi):
        return lax.dot_general(
            q, keys[lo:hi, :], (((1,), (1,)), ((), ())), preferred_element_type=F32
        )

    def get_scores(s):
        base = s * span_keys
        q = q_buf[s]
        wide = dot_keys(q, 0, base + rows)
        last = jnp.where(early, wide[:, base:], -1e30)
        wide = jnp.concatenate([wide[:, :base], last], axis=1) if s else last
        tail = jnp.where(late, dot_keys(q[half:], base + rows, base + span_keys), -1e30)
        return wide, tail

    def finish(s, wide, tail):
        base = s * span_keys
        top = jnp.max(wide, axis=1, keepdims=True)
        low_top = jnp.maximum(top[half:], jnp.max(tail, axis=1, keepdims=True))
        top = jnp.concatenate([top[:half], low_top], axis=0)
        w = jnp.exp2((wide - top) * scale)
        w_tail = jnp.exp2((tail - low_top) * scale)
        total = jnp.sum(w, axis=1, keepdims=True)
        low_total = total[half:] + jnp.sum(w_tail, axis=1, keepdims=True)
        acc = jnp.dot(w.astype(BF16), vals[0 : base + rows, :], preferred_element_type=F32)
        more = jnp.dot(
            w_tail.astype(BF16),
            vals[base + rows : base + span_keys, :],
            preferred_element_type=F32,
        )
        for lo, acc_part, sum_part in (
            (0, acc[:half], total[:half]),
            (half, acc[half:] + more, low_total),
        ):
            inv = 1.0 / (keep_rate * sum_part)
            for n in range(samples):
                done[s, n, lo : lo + half, :] = (
                    acc_part[:, n * dim : (n + 1) * dim] * inv
                ).astype(BF16)

    stage_keys(0)
    scores = get_scores(0)
    for s in range(slots):
        if s + 1 < slots:
            stage_keys(s + 1)
            ahead = get_scores(s + 1)
        stage_values(s)
        finish(s, *scores)
        scores = ahead
    sends = [pltpu.make_async_copy(done.at[me ^ i], outs[i], out_sem.at[i]) for i in range(slots)]
    for copy in sends:
        copy.start()
    for copy in sends:
        copy.wait()


def attend(lists, column, near, far, asks, ask_at, rows, tok, samples):
    slots, size, dim = column.shape
    pairs = slots * (slots + 1) // 2
    inside = pl.BlockSpec(memory_space=pltpu.VMEM)
    return pl.pallas_call(
        functools.partial(
            attend_body,
            slots=slots,
            ask_at=ask_at,
            rows=rows,
            tok=tok,
            samples=samples,
            factor=1.0 / math.sqrt(dim),
        ),
        in_specs=[pl.BlockSpec(memory_space=pltpu.SMEM)] + [inside] * (slots + 3),
        out_specs=[ANY] * slots,
        scratch_shapes=[
            pltpu.VMEM((slots * 2 * rows, dim), BF16),
            pltpu.VMEM((slots * 2 * rows, samples * dim), BF16),
            pltpu.VMEM((slots, rows, dim), BF16),
            pltpu.VMEM((slots, samples, rows, dim), BF16),
            pltpu.SemaphoreType.DMA((slots,)),
        ],
        out_shape=[jax.ShapeDtypeStruct((samples, rows, dim), BF16)] * slots,
        compiler_params=pltpu.CompilerParams(vmem_limit_bytes=LIMIT),
        cost_estimate=pl.CostEstimate(
            flops=pairs * rows * 2 * rows * dim * 2 * (1 + samples),
            bytes_accessed=2 * slots * (2 * size + samples * rows) * dim,
            transcendentals=pairs * rows * 2 * rows,
        ),
        name="attend",
    )(lists, column, near, far, *asks)


def put_body(*refs, peers, per_dev, chunk, dim):
    pieces = refs[:peers]
    out, buf, in_sem, out_sem = refs[-4:]
    me = lax.axis_index("tm")
    loads = []
    stores = []
    for i in range(peers):
        where = pl.ds(pl.multiple_of(((me ^ i) * per_dev + chunk) * dim, dim), dim)
        loads.append(pltpu.make_async_copy(pieces[i], buf.at[i], in_sem.at[i]))
        stores.append(pltpu.make_async_copy(buf.at[i], out.at[:, :, where], out_sem.at[i]))
    for copy in loads:
        copy.start()
    for load, store in zip(loads, stores):
        load.wait()
        store.start()
    for copy in stores:
        copy.wait()


def put(pieces, prior, shape, per_dev, chunk):
    peers = len(pieces)
    _, _, dim = pieces[0].shape
    args = list(pieces) if prior is None else list(pieces) + [prior]
    return pl.pallas_call(
        functools.partial(put_body, peers=peers, per_dev=per_dev, chunk=chunk, dim=dim),
        in_specs=[ANY] * len(args),
        out_specs=ANY,
        scratch_shapes=[
            pltpu.VMEM((peers,) + pieces[0].shape, BF16),
            pltpu.SemaphoreType.DMA((peers,)),
            pltpu.SemaphoreType.DMA((peers,)),
        ],
        out_shape=jax.ShapeDtypeStruct(shape, BF16),
        input_output_aliases={} if prior is None else {peers: 0},
        compiler_params=pltpu.CompilerParams(vmem_limit_bytes=LIMIT),
        cost_estimate=pl.CostEstimate(
            flops=0, bytes_accessed=4 * peers * pieces[0].size, transcendentals=0
        ),
        name="put",
    )(*args)


def per_device(queries, key_rows, value_rows, dropout, tile_lists):
    frame_dev, tok, width = queries.shape
    samples = dropout.shape[0]
    heads = dropout.shape[3]
    rows = frame_dev * tok
    peers = lax.axis_size("tm")
    per_dev = heads // peers
    space = lax.axis_size("space")
    q = queries.reshape(rows, width)
    k = key_rows.reshape(rows, width)
    v = value_rows.reshape(rows, width)
    drop = dropout.transpose(0, 3, 1, 2)
    kept = 2 * rows + BITS

    shape = (samples, rows, width)

    def spread(group):
        moved = [group[0]]
        for i in range(1, peers):
            moved.append(paired(group[i], "tm", lambda n: n ^ i))
        return moved

    def widen(packs):
        column = jnp.stack([x[:kept] for x in packs])
        near = paired(column, "space", lambda n: n ^ 1)
        far = paired(column, "space", lambda n: (((n + 1) ^ 1) - 1) % space)
        return column, near, far

    out = None
    groups = pack(q, k, v, drop, per_dev, peers, PACKAGES[:1])
    groups += pack(q, k, v, drop, per_dev, peers, PACKAGES[1:])
    packs = [spread(groups[n]) for n in range(per_dev)]
    results = []
    for chunk in range(per_dev):
        sides = widen(packs[chunk])
        source = [n for n in range(per_dev) if chunk in PACKAGES[n][1]][0]
        ask_at = kept + rows * PACKAGES[source][1].index(chunk)
        done = attend(tile_lists, *sides, packs[source], ask_at, rows, tok, samples)
        results.append(spread(done))
    for chunk in range(per_dev):
        out = put(results[chunk], out, shape, per_dev, chunk)
    return out.reshape(samples, frame_dev, tok, width)


PACKAGES = ((0, (0,)), (1, (1,)), (2, (2,)))


def solution(mesh):
    placed = (
        P("tm", "space", None),
        P("tm", "space", None),
        P("tm", "space", None),
        P(None, "tm", "space", None),
        P("space", None),
    )
    return jax.shard_map(
        per_device,
        mesh=mesh,
        in_specs=placed,
        out_specs=P(None, "tm", "space", None),
        check_vma=False,
    )
```

profile of v0, /device:TPU:1, one launch (start us, length us, event | category | flops | bytes accessed | tf_op | source)
XLA Modules:
  0.0 86.3 jit_solution(4685808181724137751)
XLA Ops:
  0.0 2.2 %pack.3 = (bf16[784,128]{1,0:T(8,128)(2,1)S(1)}, bf16[784,128]{1,0:T(8,128)(2,1)S(1)}, bf16[784,128]{1,0:T(8,128)(2,1)S(1)}, bf16[784,128]{1,0:T(8,128)(2,1)S(1)}) custom-call(bf16[256,1536]{1,0:T(8,128)(2,1)} %bitcast.29, bf16[256,1536]{1,0:T(8,128)(2,1)} %bitcast.31, bf16[256,1536]{1,0:T(8,128)(2,1)} %bitcast.33, s32[4,12,4,64]{3,2,1,0:T(4,128)} %bitcast.35), custom_call_target="tpu_custom_call" | custom-call | bytes 1605632 | tf_op jit(solution)/shard_map/pack/pallas_call | solution.py:62
  2.2 3.6 %collective-permute-start.18 = (bf16[784,128]{1,0:T(8,128)(2,1)S(1)}, bf16[784,128]{1,0:T(8,128)(2,1)S(1)}, u32[]{:S(2)}, u32[]{:S(2)}) collective-permute-start(bf16[784,128]{1,0:T(8,128)(2,1)S(1)} %get-tuple-element.48), channel_id=1, source_target_pairs={{0,192},{64,128},{128,64},{192,0},{1,193},{65,129},{129,65},{193,1... | collective-permute-start | bytes 602120 | tf_op jit(solution)/shard_map/ppermute | solution.py:23
  5.8 0.3 collective-permute-start.17
  6.2 0.3 collective-permute-start.16
  6.5 2.5 %pack.2 = (bf16[784,128]{1,0:T(8,128)(2,1)S(1)}, bf16[784,128]{1,0:T(8,128)(2,1)S(1)}, bf16[784,128]{1,0:T(8,128)(2,1)S(1)}, bf16[784,128]{1,0:T(8,128)(2,1)S(1)...) custom-call(bf16[256,1536]{1,0:T(8,128)(2,1)} %bitcast.30, ...), custom_call_target="tpu_custom_call" | custom-call | bytes 3211264 | tf_op jit(solution)/shard_map/pack/pallas_call | solution.py:62
  9.1 2.7 %collective-permute-start.10 = (bf16[784,128]{1,0:T(8,128)(2,1)S(1)}, bf16[784,128]{1,0:T(8,128)(2,1)S(1)}, u32[]{:S(2)}, u32[]{:S(2)}) collective-permute-start(bf16[784,128]{1,0:T(8,128)(2,1)S(1)} %get-tuple-element.40), channel_id=1, source_target_pairs={{0,192},{64,128},{128,64},{192,0},{1,193},{65,129},{129,65},{193,1... | collective-permute-start | bytes 602120 | tf_op jit(solution)/shard_map/ppermute | solution.py:23
  11.7 0.3 collective-permute-start.9
  12.1 3.6 %collective-permute-done.18.refs_3_ = bf16[784,128]{1,0:T(8,128)(2,1)S(1)} collective-permute-done((bf16[784,128]{1,0:T(8,128)(2,1)S(1)}, bf16[784,128]{1,0:T(8,128)(2,1)S(1)}, u32[]{:S(2)}, u32[]{:S(2)}) %collective-permute-start.18) | collective-permute-done | bytes 200736 | tf_op jit(solution)/shard_map/ppermute | solution.py:23
  15.8 4.0 %collective-permute-start.2 = (bf16[784,128]{1,0:T(8,128)(2,1)S(1)}, bf16[784,128]{1,0:T(8,128)(2,1)S(1)}, u32[]{:S(2)}, u32[]{:S(2)}) collective-permute-start(bf16[784,128]{1,0:T(8,128)(2,1)S(1)} %get-tuple-element.32), channel_id=1, source_target_pairs={{0,192},{64,128},{128,64},{192,0},{1,193},{65,129},{129,65},{193,1... | collective-permute-start | bytes 602120 | tf_op jit(solution)/shard_map/ppermute | solution.py:23
  19.8 1.3 %collective-permute-start.1 = (bf16[784,128]{1,0:T(8,128)(2,1)S(1)}, bf16[784,128]{1,0:T(8,128)(2,1)S(1)}, u32[]{:S(2)}, u32[]{:S(2)}) collective-permute-start(bf16[784,128]{1,0:T(8,128)(2,1)S(1)} %get-tuple-element.31), channel_id=1, source_target_pairs={{0,128},{64,192},{128,0},{192,64},{1,129},{65,193},{129,1},{193,65... | collective-permute-start | bytes 602120 | tf_op jit(solution)/shard_map/ppermute | solution.py:23
  21.2 2.6 %collective-permute-done.10.refs_3_ = bf16[784,128]{1,0:T(8,128)(2,1)S(1)} collective-permute-done((bf16[784,128]{1,0:T(8,128)(2,1)S(1)}, bf16[784,128]{1,0:T(8,128)(2,1)S(1)}, u32[]{:S(2)}, u32[]{:S(2)}) %collective-permute-start.10) | collective-permute-done | bytes 200736 | tf_op jit(solution)/shard_map/ppermute | solution.py:23
  23.9 4.0 %collective-permute-start.19 = (bf16[4,528,128]{2,1,0:T(8,128)(2,1)S(1)}, bf16[4,528,128]{2,1,0:T(8,128)(2,1)S(1)}, u32[]{:S(2)}, u32[]{:S(2)}) collective-permute-start(bf16[4,528,128]{2,1,0:T(8,128)(2,1)S(1)} %pad_maximum_fusion.2.column), channel_id=1, source_target_pairs={{0,1},{1,0},{2,3},{3,2},{4,5},{5,4},{6,7},{7,6},{8,9},{9,8},{10,11... | collective-permute-start | bytes 1622024 | tf_op jit(solution)/shard_map/ppermute | solution.py:23
  28.3 3.2 %collective-permute-done.2.refs_3_ = bf16[784,128]{1,0:T(8,128)(2,1)S(1)} collective-permute-done((bf16[784,128]{1,0:T(8,128)(2,1)S(1)}, bf16[784,128]{1,0:T(8,128)(2,1)S(1)}, u32[]{:S(2)}, u32[]{:S(2)}) %collective-permute-start.2) | collective-permute-done | bytes 200736 | tf_op jit(solution)/shard_map/ppermute | solution.py:23
  31.5 3.2 %collective-permute-start.11 = (bf16[4,528,128]{2,1,0:T(8,128)(2,1)S(1)}, bf16[4,528,128]{2,1,0:T(8,128)(2,1)S(1)}, u32[]{:S(2)}, u32[]{:S(2)}) collective-permute-start(bf16[4,528,128]{2,1,0:T(8,128)(2,1)S(1)} %pad_maximum_fusion.1.column), channel_id=1, source_target_pairs={{0,1},{1,0},{2,3},{3,2},{4,5},{5,4},{6,7},{7,6},{8,9},{9,8},{10,11... | collective-permute-start | bytes 1622024 | tf_op jit(solution)/shard_map/ppermute | solution.py:23
  35.1 6.5 %collective-permute-start.3 = (bf16[4,528,128]{2,1,0:T(8,128)(2,1)S(1)}, bf16[4,528,128]{2,1,0:T(8,128)(2,1)S(1)}, u32[]{:S(2)}, u32[]{:S(2)}) collective-permute-start(bf16[4,528,128]{2,1,0:T(8,128)(2,1)S(1)} %pad_maximum_fusion.column), channel_id=1, source_target_pairs={{0,1},{1,0},{2,3},{3,2},{4,5},{5,4},{6,7},{7,6},{8,9},{9,8},{10,11... | collective-permute-start | bytes 1622024 | tf_op jit(solution)/shard_map/ppermute | solution.py:23
  41.6 3.6 %attend.5 = (bf16[4,256,128]{2,1,0:T(8,128)(2,1)S(1)}, bf16[4,256,128]{2,1,0:T(8,128)(2,1)S(1)}, bf16[4,256,128]{2,1,0:T(8,128)(2,1)S(1)}, bf16[4,256,128]{2,1,0:T(8,128)(2,1)S(1)}) custom-call(s32[1,2]{1,0:T(1,128)S(1)} %copy-done, bf16[4,528,128]{2,1,0:T(8,128)(2,1)S(1)} %pad_maximum_fusion.2.column, ...), custom_call_target="tpu_custom_call" | custom-call | flops 1677721600 | bytes 2129920 | tf_op jit(solution)/shard_map/attend/pallas_call | solution.py:185
  45.2 0.5 collective-permute-start.21
  45.7 3.9 %collective-permute-start.22 = (bf16[4,256,128]{2,1,0:T(8,128)(2,1)S(1)}, bf16[4,256,128]{2,1,0:T(8,128)(2,1)S(1)}, u32[]{:S(2)}, u32[]{:S(2)}) collective-permute-start(bf16[4,256,128]{2,1,0:T(8,128)(2,1)S(1)} %get-tuple-element.51), channel_id=1, source_target_pairs={{0,128},{64,192},{128,0},{192,64},{1,129},{65,193},{129,1},{193,65... | collective-permute-start | bytes 786440 | tf_op jit(solution)/shard_map/ppermute | solution.py:23
  49.5 3.6 %attend.4 = (bf16[4,256,128]{2,1,0:T(8,128)(2,1)S(1)}, bf16[4,256,128]{2,1,0:T(8,128)(2,1)S(1)}, bf16[4,256,128]{2,1,0:T(8,128)(2,1)S(1)}, bf16[4,256,128]{2,1,0:T(8,128)(2,1)S(1)}) custom-call(s32[1,2]{1,0:T(1,128)S(1)} %copy-done, bf16[4,528,128]{2,1,0:T(8,128)(2,1)S(1)} %pad_maximum_fusion.1.column, ...), custom_call_target="tpu_custom_call" | custom-call | flops 1677721600 | bytes 2129920 | tf_op jit(solution)/shard_map/attend/pallas_call | solution.py:185
  53.3 3.9 %collective-permute-start.14 = (bf16[4,256,128]{2,1,0:T(8,128)(2,1)S(1)}, bf16[4,256,128]{2,1,0:T(8,128)(2,1)S(1)}, u32[]{:S(2)}, u32[]{:S(2)}) collective-permute-start(bf16[4,256,128]{2,1,0:T(8,128)(2,1)S(1)} %get-tuple-element.43), channel_id=1, source_target_pairs={{0,128},{64,192},{128,0},{192,64},{1,129},{65,193},{129,1},{193,65... | collective-permute-start | bytes 786440 | tf_op jit(solution)/shard_map/ppermute | solution.py:23
  57.1 3.6 %attend.3 = (bf16[4,256,128]{2,1,0:T(8,128)(2,1)S(1)}, bf16[4,256,128]{2,1,0:T(8,128)(2,1)S(1)}, bf16[4,256,128]{2,1,0:T(8,128)(2,1)S(1)}, bf16[4,256,128]{2,1,0:T(8,128)(2,1)S(1)}) custom-call(s32[1,2]{1,0:T(1,128)S(1)} %copy-done, bf16[4,528,128]{2,1,0:T(8,128)(2,1)S(1)} %pad_maximum_fusion.column, bf16[4,528,128]{2,1,0:T(8,128)(2,1)S(1)} %collective-permute-done.3.near, ...), custom_call_target="tpu_custom_call" | custom-call | flops 1677721600 | bytes 2129920 | tf_op jit(solution)/shard_map/attend/pallas_call | solution.py:185
  61.0 1.3 %collective-permute-done.23.refs_3_ = bf16[4,256,128]{2,1,0:T(8,128)(2,1)S(1)} collective-permute-done((bf16[4,256,128]{2,1,0:T(8,128)(2,1)S(1)}, bf16[4,256,128]{2,1,0:T(8,128)(2,1)S(1)}, u32[]{:S(2)}, u32[]{:S(2)}) %collective-permute-start.23) | collective-permute-done | bytes 262176 | tf_op jit(solution)/shard_map/ppermute | solution.py:23
  62.3 2.4 %collective-permute-start.6 = (bf16[4,256,128]{2,1,0:T(8,128)(2,1)S(1)}, bf16[4,256,128]{2,1,0:T(8,128)(2,1)S(1)}, u32[]{:S(2)}, u32[]{:S(2)}) collective-permute-start(bf16[4,256,128]{2,1,0:T(8,128)(2,1)S(1)} %get-tuple-element.35), channel_id=1, source_target_pairs={{0,128},{64,192},{128,0},{192,64},{1,129},{65,193},{129,1},{193,65... | collective-permute-start | bytes 786440 | tf_op jit(solution)/shard_map/ppermute | solution.py:23
  64.7 1.7 %collective-permute-start.7 = (bf16[4,256,128]{2,1,0:T(8,128)(2,1)S(1)}, bf16[4,256,128]{2,1,0:T(8,128)(2,1)S(1)}, u32[]{:S(2)}, u32[]{:S(2)}) collective-permute-start(bf16[4,256,128]{2,1,0:T(8,128)(2,1)S(1)} %get-tuple-element.36), channel_id=1, source_target_pairs={{0,192},{64,128},{128,64},{192,0},{1,193},{65,129},{129,65},{193,1... | collective-permute-start | bytes 786440 | tf_op jit(solution)/shard_map/ppermute | solution.py:23
  66.4 1.1 %put.3.refs_4_ = bf16[4,256,1536]{2,1,0:T(8,128)(2,1)} custom-call(bf16[4,256,128]{2,1,0:T(8,128)(2,1)S(1)} %get-tuple-element.49.refs_0_, bf16[4,256,128]{2,1,0:T(8,128)(2,1)S(1)} %collective-permute-done.21.refs_1_, bf16[4,256,128]{2,1,0:T(8,128)(2,1)S(1)} %collective-permute-done.22.refs_2_, bf16[4,256,128]{2,1,0:T(8,128)(2,1)S(1)} %collective-permute-done.23.refs_3_), custom_call_target="tpu_custom_call" | custom-call | bytes 2097152 | tf_op jit(solution)/shard_map/put/pallas_call | solution.py:238
  67.5 4.3 %collective-permute-done.14.refs_2_ = bf16[4,256,128]{2,1,0:T(8,128)(2,1)S(1)} collective-permute-done((bf16[4,256,128]{2,1,0:T(8,128)(2,1)S(1)}, bf16[4,256,128]{2,1,0:T(8,128)(2,1)S(1)}, u32[]{:S(2)}, u32[]{:S(2)}) %collective-permute-start.14) | collective-permute-done | bytes 262176 | tf_op jit(solution)/shard_map/ppermute | solution.py:23
  71.8 1.0 %collective-permute-done.15.refs_3_ = bf16[4,256,128]{2,1,0:T(8,128)(2,1)S(1)} collective-permute-done((bf16[4,256,128]{2,1,0:T(8,128)(2,1)S(1)}, bf16[4,256,128]{2,1,0:T(8,128)(2,1)S(1)}, u32[]{:S(2)}, u32[]{:S(2)}) %collective-permute-start.15) | collective-permute-done | bytes 262176 | tf_op jit(solution)/shard_map/ppermute | solution.py:23
  72.7 1.1 %put.4.refs_4_ = bf16[4,256,1536]{2,1,0:T(8,128)(2,1)} custom-call(bf16[4,256,128]{2,1,0:T(8,128)(2,1)S(1)} %get-tuple-element.41.refs_0_, bf16[4,256,128]{2,1,0:T(8,128)(2,1)S(1)} %collective-permute-done.13.refs_1_, bf16[4,256,128]{2,1,0:T(8,128)(2,1)S(1)} %collective-permute-done.14.refs_2_, ...), custom_call_target="tpu_custom_call", output_to_operand_aliasing={{}: (4, {})} | custom-call | bytes 2097152 | tf_op jit(solution)/shard_map/put/pallas_call | solution.py:238
  73.9 0.9 %collective-permute-done.5.refs_1_ = bf16[4,256,128]{2,1,0:T(8,128)(2,1)S(1)} collective-permute-done((bf16[4,256,128]{2,1,0:T(8,128)(2,1)S(1)}, bf16[4,256,128]{2,1,0:T(8,128)(2,1)S(1)}, u32[]{:S(2)}, u32[]{:S(2)}) %collective-permute-start.5) | collective-permute-done | bytes 262176 | tf_op jit(solution)/shard_map/ppermute | solution.py:23
  74.8 8.3 %collective-permute-done.6.refs_2_ = bf16[4,256,128]{2,1,0:T(8,128)(2,1)S(1)} collective-permute-done((bf16[4,256,128]{2,1,0:T(8,128)(2,1)S(1)}, bf16[4,256,128]{2,1,0:T(8,128)(2,1)S(1)}, u32[]{:S(2)}, u32[]{:S(2)}) %collective-permute-start.6) | collective-permute-done | bytes 262176 | tf_op jit(solution)/shard_map/ppermute | solution.py:23
  83.1 2.0 %collective-permute-done.7.refs_3_ = bf16[4,256,128]{2,1,0:T(8,128)(2,1)S(1)} collective-permute-done((bf16[4,256,128]{2,1,0:T(8,128)(2,1)S(1)}, bf16[4,256,128]{2,1,0:T(8,128)(2,1)S(1)}, u32[]{:S(2)}, u32[]{:S(2)}) %collective-permute-start.7) | collective-permute-done | bytes 262176 | tf_op jit(solution)/shard_map/ppermute | solution.py:23
  85.1 1.1 %put.5 = bf16[4,256,1536]{2,1,0:T(8,128)(2,1)} custom-call(bf16[4,256,128]{2,1,0:T(8,128)(2,1)S(1)} %get-tuple-element.33.refs_0_, bf16[4,256,128]{2,1,0:T(8,128)(2,1)S(1)} %collective-permute-done.5.refs_1_, bf16[4,256,128]{2,1,0:T(8,128)(2,1)S(1)} %collective-permute-done.6.refs_2_, ...), custom_call_target="tpu_custom_call", output_to_operand_aliasing={{}: (4, {})} | custom-call | bytes 2097152 | tf_op jit(solution)/shard_map/put/pallas_call | solution.py:238
  (41 shorter events, 1.2 us)
Async XLA Ops:
  2.2 13.6 %collective-permute-start.18 = (bf16[784,128]{1,0:T(8,128)(2,1)S(1)}, bf16[784,128]{1,0:T(8,128)(2,1)S(1)}, u32[]{:S(2)}, u32[]{:S(2)}) collective-permute-start(bf16[784,128]{1,0:T(8,128)(2,1)S(1)} %get-tuple-element.48), channel_id=1, source_target_pairs={{0,192},{64,128},{128,64},{192,0},{1,193},{65,129},{129,65},{193,1... | collective-permute-start | bytes 602120 | tf_op jit(solution)/shard_map/ppermute | solution.py:23
  5.8 10.0 %collective-permute-start.17 = (bf16[784,128]{1,0:T(8,128)(2,1)S(1)}, bf16[784,128]{1,0:T(8,128)(2,1)S(1)}, u32[]{:S(2)}, u32[]{:S(2)}) collective-permute-start(bf16[784,128]{1,0:T(8,128)(2,1)S(1)} %get-tuple-element.47), channel_id=1, source_target_pairs={{0,128},{64,192},{128,0},{192,64},{1,129},{65,193},{129,1},{193,65... | collective-permute-start | bytes 602120 | tf_op jit(solution)/shard_map/ppermute | solution.py:23
  6.2 13.6 %collective-permute-start.16 = (bf16[784,128]{1,0:T(8,128)(2,1)S(1)}, bf16[784,128]{1,0:T(8,128)(2,1)S(1)}, u32[]{:S(2)}, u32[]{:S(2)}) collective-permute-start(bf16[784,128]{1,0:T(8,128)(2,1)S(1)} %get-tuple-element.46), channel_id=1, source_target_pairs={{0,64},{64,0},{128,192},{192,128},{1,65},{65,1},{129,193},{193,129... | collective-permute-start | bytes 602120 | tf_op jit(solution)/shard_map/ppermute | solution.py:23
  9.1 14.8 %collective-permute-start.10 = (bf16[784,128]{1,0:T(8,128)(2,1)S(1)}, bf16[784,128]{1,0:T(8,128)(2,1)S(1)}, u32[]{:S(2)}, u32[]{:S(2)}) collective-permute-start(bf16[784,128]{1,0:T(8,128)(2,1)S(1)} %get-tuple-element.40), channel_id=1, source_target_pairs={{0,192},{64,128},{128,64},{192,0},{1,193},{65,129},{129,65},{193,1... | collective-permute-start | bytes 602120 | tf_op jit(solution)/shard_map/ppermute | solution.py:23
  11.7 12.1 %collective-permute-start.9 = (bf16[784,128]{1,0:T(8,128)(2,1)S(1)}, bf16[784,128]{1,0:T(8,128)(2,1)S(1)}, u32[]{:S(2)}, u32[]{:S(2)}) collective-permute-start(bf16[784,128]{1,0:T(8,128)(2,1)S(1)} %get-tuple-element.39), channel_id=1, source_target_pairs={{0,128},{64,192},{128,0},{192,64},{1,129},{65,193},{129,1},{193,65... | collective-permute-start | bytes 602120 | tf_op jit(solution)/shard_map/ppermute | solution.py:23
  12.1 29.5 %copy-start = (s32[1,2]{1,0:T(1,128)S(1)}, s32[1,2]{1,0:T(1,128)}, u32[]{:S(2)}) copy-start(s32[1,2]{1,0:T(1,128)} %lists.5) | copy-start | bytes 28
  15.8 12.1 %collective-permute-start.8 = (bf16[784,128]{1,0:T(8,128)(2,1)S(1)}, bf16[784,128]{1,0:T(8,128)(2,1)S(1)}, u32[]{:S(2)}, u32[]{:S(2)}) collective-permute-start(bf16[784,128]{1,0:T(8,128)(2,1)S(1)} %get-tuple-element.38), channel_id=1, source_target_pairs={{0,64},{64,0},{128,192},{192,128},{1,65},{65,1},{129,193},{193,129... | collective-permute-start | bytes 602120 | tf_op jit(solution)/shard_map/ppermute | solution.py:23
  15.8 15.7 %collective-permute-start.2 = (bf16[784,128]{1,0:T(8,128)(2,1)S(1)}, bf16[784,128]{1,0:T(8,128)(2,1)S(1)}, u32[]{:S(2)}, u32[]{:S(2)}) collective-permute-start(bf16[784,128]{1,0:T(8,128)(2,1)S(1)} %get-tuple-element.32), channel_id=1, source_target_pairs={{0,192},{64,128},{128,64},{192,0},{1,193},{65,129},{129,65},{193,1... | collective-permute-start | bytes 602120 | tf_op jit(solution)/shard_map/ppermute | solution.py:23
  19.8 14.9 %collective-permute-start.1 = (bf16[784,128]{1,0:T(8,128)(2,1)S(1)}, bf16[784,128]{1,0:T(8,128)(2,1)S(1)}, u32[]{:S(2)}, u32[]{:S(2)}) collective-permute-start(bf16[784,128]{1,0:T(8,128)(2,1)S(1)} %get-tuple-element.31), channel_id=1, source_target_pairs={{0,128},{64,192},{128,0},{192,64},{1,129},{65,193},{129,1},{193,65... | collective-permute-start | bytes 602120 | tf_op jit(solution)/shard_map/ppermute | solution.py:23
  23.8 11.1 %collective-permute-start = (bf16[784,128]{1,0:T(8,128)(2,1)S(1)}, bf16[784,128]{1,0:T(8,128)(2,1)S(1)}, u32[]{:S(2)}, u32[]{:S(2)}) collective-permute-start(bf16[784,128]{1,0:T(8,128)(2,1)S(1)} %get-tuple-element.30), channel_id=1, source_target_pairs={{0,64},{64,0},{128,192},{192,128},{1,65},{65,1},{129,193},{193,129... | collective-permute-start | bytes 602120 | tf_op jit(solution)/shard_map/ppermute | solution.py:23
  23.9 17.7 %collective-permute-start.19 = (bf16[4,528,128]{2,1,0:T(8,128)(2,1)S(1)}, bf16[4,528,128]{2,1,0:T(8,128)(2,1)S(1)}, u32[]{:S(2)}, u32[]{:S(2)}) collective-permute-start(bf16[4,528,128]{2,1,0:T(8,128)(2,1)S(1)} %pad_maximum_fusion.2.column), channel_id=1, source_target_pairs={{0,1},{1,0},{2,3},{3,2},{4,5},{5,4},{6,7},{7,6},{8,9},{9,8},{10,11... | collective-permute-start | bytes 1622024 | tf_op jit(solution)/shard_map/ppermute | solution.py:23
  27.9 13.7 %collective-permute-start.20 = (bf16[4,528,128]{2,1,0:T(8,128)(2,1)S(1)}, bf16[4,528,128]{2,1,0:T(8,128)(2,1)S(1)}, u32[]{:S(2)}, u32[]{:S(2)}) collective-permute-start(bf16[4,528,128]{2,1,0:T(8,128)(2,1)S(1)} %pad_maximum_fusion.2.column), channel_id=1, source_target_pairs={{0,63},{1,2},{2,1},{3,4},{4,3},{5,6},{6,5},{7,8},{8,7},{9,10},{10,... | collective-permute-start | bytes 1622024 | tf_op jit(solution)/shard_map/ppermute | solution.py:23
  31.5 14.2 %collective-permute-start.11 = (bf16[4,528,128]{2,1,0:T(8,128)(2,1)S(1)}, bf16[4,528,128]{2,1,0:T(8,128)(2,1)S(1)}, u32[]{:S(2)}, u32[]{:S(2)}) collective-permute-start(bf16[4,528,128]{2,1,0:T(8,128)(2,1)S(1)} %pad_maximum_fusion.1.column), channel_id=1, source_target_pairs={{0,1},{1,0},{2,3},{3,2},{4,5},{5,4},{6,7},{7,6},{8,9},{9,8},{10,11... | collective-permute-start | bytes 1622024 | tf_op jit(solution)/shard_map/ppermute | solution.py:23
  34.7 14.8 %collective-permute-start.12 = (bf16[4,528,128]{2,1,0:T(8,128)(2,1)S(1)}, bf16[4,528,128]{2,1,0:T(8,128)(2,1)S(1)}, u32[]{:S(2)}, u32[]{:S(2)}) collective-permute-start(bf16[4,528,128]{2,1,0:T(8,128)(2,1)S(1)} %pad_maximum_fusion.1.column), channel_id=1, source_target_pairs={{0,63},{1,2},{2,1},{3,4},{4,3},{5,6},{6,5},{7,8},{8,7},{9,10},{10,... | collective-permute-start | bytes 1622024 | tf_op jit(solution)/shard_map/ppermute | solution.py:23
  35.1 18.1 %collective-permute-start.3 = (bf16[4,528,128]{2,1,0:T(8,128)(2,1)S(1)}, bf16[4,528,128]{2,1,0:T(8,128)(2,1)S(1)}, u32[]{:S(2)}, u32[]{:S(2)}) collective-permute-start(bf16[4,528,128]{2,1,0:T(8,128)(2,1)S(1)} %pad_maximum_fusion.column), channel_id=1, source_target_pairs={{0,1},{1,0},{2,3},{3,2},{4,5},{5,4},{6,7},{7,6},{8,9},{9,8},{10,11... | collective-permute-start | bytes 1622024 | tf_op jit(solution)/shard_map/ppermute | solution.py:23
  41.6 11.7 %collective-permute-start.4 = (bf16[4,528,128]{2,1,0:T(8,128)(2,1)S(1)}, bf16[4,528,128]{2,1,0:T(8,128)(2,1)S(1)}, u32[]{:S(2)}, u32[]{:S(2)}) collective-permute-start(bf16[4,528,128]{2,1,0:T(8,128)(2,1)S(1)} %pad_maximum_fusion.column), channel_id=1, source_target_pairs={{0,63},{1,2},{2,1},{3,4},{4,3},{5,6},{6,5},{7,8},{8,7},{9,10},{10,... | collective-permute-start | bytes 1622024 | tf_op jit(solution)/shard_map/ppermute | solution.py:23
  45.2 15.5 %collective-permute-start.21 = (bf16[4,256,128]{2,1,0:T(8,128)(2,1)S(1)}, bf16[4,256,128]{2,1,0:T(8,128)(2,1)S(1)}, u32[]{:S(2)}, u32[]{:S(2)}) collective-permute-start(bf16[4,256,128]{2,1,0:T(8,128)(2,1)S(1)} %get-tuple-element.50), channel_id=1, source_target_pairs={{0,64},{64,0},{128,192},{192,128},{1,65},{65,1},{129,193},{193,129... | collective-permute-start | bytes 786440 | tf_op jit(solution)/shard_map/ppermute | solution.py:23
  45.7 15.2 %collective-permute-start.22 = (bf16[4,256,128]{2,1,0:T(8,128)(2,1)S(1)}, bf16[4,256,128]{2,1,0:T(8,128)(2,1)S(1)}, u32[]{:S(2)}, u32[]{:S(2)}) collective-permute-start(bf16[4,256,128]{2,1,0:T(8,128)(2,1)S(1)} %get-tuple-element.51), channel_id=1, source_target_pairs={{0,128},{64,192},{128,0},{192,64},{1,129},{65,193},{129,1},{193,65... | collective-permute-start | bytes 786440 | tf_op jit(solution)/shard_map/ppermute | solution.py:23
  49.5 12.7 %collective-permute-start.23 = (bf16[4,256,128]{2,1,0:T(8,128)(2,1)S(1)}, bf16[4,256,128]{2,1,0:T(8,128)(2,1)S(1)}, u32[]{:S(2)}, u32[]{:S(2)}) collective-permute-start(bf16[4,256,128]{2,1,0:T(8,128)(2,1)S(1)} %get-tuple-element.52), channel_id=1, source_target_pairs={{0,192},{64,128},{128,64},{192,0},{1,193},{65,129},{129,65},{193,1... | collective-permute-start | bytes 786440 | tf_op jit(solution)/shard_map/ppermute | solution.py:23
  53.2 11.6 %collective-permute-start.13 = (bf16[4,256,128]{2,1,0:T(8,128)(2,1)S(1)}, bf16[4,256,128]{2,1,0:T(8,128)(2,1)S(1)}, u32[]{:S(2)}, u32[]{:S(2)}) collective-permute-start(bf16[4,256,128]{2,1,0:T(8,128)(2,1)S(1)} %get-tuple-element.42), channel_id=1, source_target_pairs={{0,64},{64,0},{128,192},{192,128},{1,65},{65,1},{129,193},{193,129... | collective-permute-start | bytes 786440 | tf_op jit(solution)/shard_map/ppermute | solution.py:23
  53.3 18.5 %collective-permute-start.14 = (bf16[4,256,128]{2,1,0:T(8,128)(2,1)S(1)}, bf16[4,256,128]{2,1,0:T(8,128)(2,1)S(1)}, u32[]{:S(2)}, u32[]{:S(2)}) collective-permute-start(bf16[4,256,128]{2,1,0:T(8,128)(2,1)S(1)} %get-tuple-element.43), channel_id=1, source_target_pairs={{0,128},{64,192},{128,0},{192,64},{1,129},{65,193},{129,1},{193,65... | collective-permute-start | bytes 786440 | tf_op jit(solution)/shard_map/ppermute | solution.py:23
  60.8 12.0 %collective-permute-start.15 = (bf16[4,256,128]{2,1,0:T(8,128)(2,1)S(1)}, bf16[4,256,128]{2,1,0:T(8,128)(2,1)S(1)}, u32[]{:S(2)}, u32[]{:S(2)}) collective-permute-start(bf16[4,256,128]{2,1,0:T(8,128)(2,1)S(1)} %get-tuple-element.44), channel_id=1, source_target_pairs={{0,192},{64,128},{128,64},{192,0},{1,193},{65,129},{129,65},{193,1... | collective-permute-start | bytes 786440 | tf_op jit(solution)/shard_map/ppermute | solution.py:23
  60.9 13.9 %collective-permute-start.5 = (bf16[4,256,128]{2,1,0:T(8,128)(2,1)S(1)}, bf16[4,256,128]{2,1,0:T(8,128)(2,1)S(1)}, u32[]{:S(2)}, u32[]{:S(2)}) collective-permute-start(bf16[4,256,128]{2,1,0:T(8,128)(2,1)S(1)} %get-tuple-element.34), channel_id=1, source_target_pairs={{0,64},{64,0},{128,192},{192,128},{1,65},{65,1},{129,193},{193,129... | collective-permute-start | bytes 786440 | tf_op jit(solution)/shard_map/ppermute | solution.py:23
  62.3 20.8 %collective-permute-start.6 = (bf16[4,256,128]{2,1,0:T(8,128)(2,1)S(1)}, bf16[4,256,128]{2,1,0:T(8,128)(2,1)S(1)}, u32[]{:S(2)}, u32[]{:S(2)}) collective-permute-start(bf16[4,256,128]{2,1,0:T(8,128)(2,1)S(1)} %get-tuple-element.35), channel_id=1, source_target_pairs={{0,128},{64,192},{128,0},{192,64},{1,129},{65,193},{129,1},{193,65... | collective-permute-start | bytes 786440 | tf_op jit(solution)/shard_map/ppermute | solution.py:23
  64.7 20.4 %collective-permute-start.7 = (bf16[4,256,128]{2,1,0:T(8,128)(2,1)S(1)}, bf16[4,256,128]{2,1,0:T(8,128)(2,1)S(1)}, u32[]{:S(2)}, u32[]{:S(2)}) collective-permute-start(bf16[4,256,128]{2,1,0:T(8,128)(2,1)S(1)} %get-tuple-element.36), channel_id=1, source_target_pairs={{0,192},{64,128},{128,64},{192,0},{1,193},{65,129},{129,65},{193,1... | collective-permute-start | bytes 786440 | tf_op jit(solution)/shard_map/ppermute | solution.py:23
where the time goes:
time: 86.6 us; the launch traced here: 86.3 us
  starting transfers between devices  39.4 us (45%)
  waiting for transfers between devices  27.3 us (32%)
  Pallas kernels  18.8 us (22%)
    ppermute x24, starting transfers between devices, paired(): lax.ppermute(x, axis, [(i, mate(i)) for i in range(lax.axis_size(axis))])  39.4 us
    ppermute x24, waiting for transfers between devices, paired(): lax.ppermute(x, axis, [(i, mate(i)) for i in range(lax.axis_size(axis))])  27.3 us
    pallas_call x3, Pallas kernels, attend(): pl.pallas_call(functools.partial(attend_body, slots=slots, ask_at=ask_at,...  10.8 us
    pallas_call x2, Pallas kernels, pack(): pl.pallas_call(functools.partial(pack_body, peers=peers, per_dev=per_dev,...  4.72 us
    pallas_call x3, Pallas kernels, put(): pl.pallas_call(functools.partial(put_body, peers=peers, per_dev=per_dev,...  3.31 us
  transfers between devices with their start and end apart: 24, of which 9 were waited for; matrix products, arithmetic and copies ran while one was open for 0% of the time, Pallas kernels for 18%

commit v1 on v0

--- a/solution.py
+++ b/solution.py
@@ -30,7 +30,7 @@
 
 def pack_body(q, k, v, drop, *refs, peers, per_dev, packages, rows, dim):
     outs = refs[: peers * len(packages)]
-    in_sem = refs[-1]
+    flags, in_sem, flag_sem = refs[peers * len(packages) :]
     me = lax.axis_index("tm")
     zero = jnp.zeros((BITS, dim - drop.shape[3]), BF16)
     plan = [(n, i) for n in range(len(packages)) for i in tuple(range(1, peers)) + (0,)]
@@ -46,8 +46,14 @@
                 pltpu.make_async_copy(x.at[:, where], out.at[pl.ds(at, rows)], in_sem.at[n, i, m])
             )
             loads[-1].start()
+    flag_loads = {}
     for n, i in plan:
-        bits = drop[:, (me ^ i) * per_dev + packages[n][0]].reshape(BITS, drop.shape[3])
+        head = (me ^ i) * per_dev + packages[n][0]
+        flag_loads[n, i] = pltpu.make_async_copy(drop.at[:, head], flags.at[n, i], flag_sem.at[n, i])
+        flag_loads[n, i].start()
+    for n, i in plan:
+        flag_loads[n, i].wait()
+        bits = flags[n, i].reshape(BITS, drop.shape[3])
         outs[n * peers + i][2 * rows : 2 * rows + BITS, :] = jnp.concatenate(
             [bits.astype(F32).astype(BF16), zero], axis=1
         )
@@ -63,10 +69,12 @@
         functools.partial(
             pack_body, peers=peers, per_dev=per_dev, packages=packages, rows=rows, dim=dim
         ),
-        in_specs=[HBM, HBM, HBM, pl.BlockSpec(memory_space=pltpu.VMEM)],
+        in_specs=[HBM] * 4,
         out_specs=[pl.BlockSpec(memory_space=pltpu.VMEM)] * len(sizes),
         scratch_shapes=[
-            pltpu.SemaphoreType.DMA((len(packages), peers, 2 + max(len(p[1]) for p in packages)))
+            pltpu.VMEM((len(packages), peers, drop.shape[0]) + drop.shape[2:], drop.dtype),
+            pltpu.SemaphoreType.DMA((len(packages), peers, 2 + max(len(p[1]) for p in packages))),
+            pltpu.SemaphoreType.DMA((len(packages), peers)),
         ],
         out_shape=[pltpu.VMEM((size, dim), BF16) for size in sizes],
         compiler_params=pltpu.CompilerParams(vmem_limit_bytes=PACK_LIMIT),
@@ -212,16 +220,16 @@
     )(lists, column, near, far, *asks)
 
 
-def put_body(*refs, peers, per_dev, chunk, dim):
-    pieces = refs[:peers]
+def put_body(*refs, slots, per_dev, chunk, dim):
+    pieces = refs[: len(slots)]
     out, buf, in_sem, out_sem = refs[-4:]
     me = lax.axis_index("tm")
     loads = []
     stores = []
-    for i in range(peers):
+    for n, i in enumerate(slots):
         where = pl.ds(pl.multiple_of(((me ^ i) * per_dev + chunk) * dim, dim), dim)
-        loads.append(pltpu.make_async_copy(pieces[i], buf.at[i], in_sem.at[i]))
-        stores.append(pltpu.make_async_copy(buf.at[i], out.at[:, :, where], out_sem.at[i]))
+        loads.append(pltpu.make_async_copy(pieces[n], buf.at[n], in_sem.at[n]))
+        stores.append(pltpu.make_async_copy(buf.at[n], out.at[:, :, where], out_sem.at[n]))
     for copy in loads:
         copy.start()
     for load, store in zip(loads, stores):
@@ -231,12 +239,13 @@
         copy.wait()
 
 
-def put(pieces, prior, shape, per_dev, chunk):
+def put(pieces, slots, prior, shape, per_dev, chunk):
+    pieces = [pieces[i] for i in slots]
     peers = len(pieces)
     _, _, dim = pieces[0].shape
     args = list(pieces) if prior is None else list(pieces) + [prior]
     return pl.pallas_call(
-        functools.partial(put_body, peers=peers, per_dev=per_dev, chunk=chunk, dim=dim),
+        functools.partial(put_body, slots=slots, per_dev=per_dev, chunk=chunk, dim=dim),
         in_specs=[ANY] * len(args),
         out_specs=ANY,
         scratch_shapes=[
@@ -293,12 +302,15 @@
         ask_at = kept + rows * PACKAGES[source][1].index(chunk)
         done = attend(tile_lists, *sides, packs[source], ask_at, rows, tok, samples)
         results.append(spread(done))
-    for chunk in range(per_dev):
-        out = put(results[chunk], out, shape, per_dev, chunk)
+    for chunk, slots in PUTS:
+        out = put(results[chunk], slots, out, shape, per_dev, chunk)
     return out.reshape(samples, frame_dev, tok, width)
 
 
-PACKAGES = ((0, (0,)), (1, (1,)), (2, (2,)))
+PACKAGES = ((0, ()), (1, (0,)), (2, (1, 2)))
+
+
+PUTS = ((0, (0, 1, 2, 3)), (1, (0, 1, 2, 3)), (2, (0, 1)), (2, (3, 2)))
 
 
 def solution(mesh):

time: 86.6 us -> 85.6 us (0.988)
  the two profiles are of different devices: /device:TPU:1 before, /device:TPU:24 now
where the time goes in v1:
time: 85.6 us; the launch traced here: 85.4 us
  starting transfers between devices  40.1 us (47%)
  waiting for transfers between devices  26.8 us (31%)
  Pallas kernels  17.9 us (21%)
    ppermute x24, starting transfers between devices, paired(): lax.ppermute(x, axis, [(i, mate(i)) for i in range(lax.axis_size(axis))])  40.1 us
    ppermute x24, waiting for transfers between devices, paired(): lax.ppermute(x, axis, [(i, mate(i)) for i in range(lax.axis_size(axis))])  26.8 us
    pallas_call x3, Pallas kernels, attend(): pl.pallas_call(functools.partial(attend_body, slots=slots, ask_at=ask_at,...  10.8 us
    pallas_call x4, Pallas kernels, put(): pl.pallas_call(functools.partial(put_body, slots=slots, per_dev=per_dev,...  3.94 us
    pallas_call x2, Pallas kernels, pack(): pl.pallas_call(functools.partial(pack_body, peers=peers, per_dev=per_dev,...  3.12 us
  transfers between devices with their start and end apart: 24, of which 10 were waited for; matrix products, arithmetic and copies ran while one was open for 0% of the time, Pallas kernels for 19%

profile of v1, /device:TPU:24, one launch (start us, length us, event | category | flops | bytes accessed | tf_op | source)
XLA Modules:
  0.0 85.4 jit_solution(1030262655098478818)
XLA Ops:
  0.0 1.2 %pack.3 = (bf16[528,128]{1,0:T(8,128)(2,1)S(1)}, bf16[528,128]{1,0:T(8,128)(2,1)S(1)}, bf16[528,128]{1,0:T(8,128)(2,1)S(1)}, bf16[528,128]{1,0:T(8,128)(2,1)S(1)}) custom-call(bf16[256,1536]{1,0:T(8,128)(2,1)} %bitcast.26, bf16[256,1536]{1,0:T(8,128)(2,1)} %bitcast.28, bf16[256,1536]{1,0:T(8,128)(2,1)} %bitcast.30, s32[4,12,4,64]{3,2,1,0:T(4,128)} %bitcast.32), custom_call_target="tpu_custom_call" | custom-call | bytes 1081344 | tf_op jit(solution)/shard_map/pack/pallas_call | solution.py:68
  1.2 0.8 collective-permute-start.16
  2.1 2.6 %collective-permute-start.17 = (bf16[528,128]{1,0:T(8,128)(2,1)S(1)}, bf16[528,128]{1,0:T(8,128)(2,1)S(1)}, u32[]{:S(2)}, u32[]{:S(2)}) collective-permute-start(bf16[528,128]{1,0:T(8,128)(2,1)S(1)} %get-tuple-element.47), channel_id=1, source_target_pairs={{0,128},{64,192},{128,0},{192,64},{1,129},{65,193},{129,1},{193,65... | collective-permute-start | bytes 405512 | tf_op jit(solution)/shard_map/ppermute | solution.py:23
  4.7 1.3 %collective-permute-start.18 = (bf16[528,128]{1,0:T(8,128)(2,1)S(1)}, bf16[528,128]{1,0:T(8,128)(2,1)S(1)}, u32[]{:S(2)}, u32[]{:S(2)}) collective-permute-start(bf16[528,128]{1,0:T(8,128)(2,1)S(1)} %get-tuple-element.48), channel_id=1, source_target_pairs={{0,192},{64,128},{128,64},{192,0},{1,193},{65,129},{129,65},{193,1... | collective-permute-start | bytes 405512 | tf_op jit(solution)/shard_map/ppermute | solution.py:23
  6.0 1.9 %pack.2 = (bf16[784,128]{1,0:T(8,128)(2,1)S(1)}, bf16[784,128]{1,0:T(8,128)(2,1)S(1)}, bf16[784,128]{1,0:T(8,128)(2,1)S(1)}, bf16[784,128]{1,0:T(8,128)(2,1)S(1)...) custom-call(bf16[256,1536]{1,0:T(8,128)(2,1)} %bitcast.27, ...), custom_call_target="tpu_custom_call" | custom-call | bytes 3735552 | tf_op jit(solution)/shard_map/pack/pallas_call | solution.py:68
  8.0 3.4 %collective-permute-start.9 = (bf16[784,128]{1,0:T(8,128)(2,1)S(1)}, bf16[784,128]{1,0:T(8,128)(2,1)S(1)}, u32[]{:S(2)}, u32[]{:S(2)}) collective-permute-start(bf16[784,128]{1,0:T(8,128)(2,1)S(1)} %get-tuple-element.39), channel_id=1, source_target_pairs={{0,128},{64,192},{128,0},{192,64},{1,129},{65,193},{129,1},{193,65... | collective-permute-start | bytes 602120 | tf_op jit(solution)/shard_map/ppermute | solution.py:23
  11.5 1.4 %collective-permute-start.10 = (bf16[784,128]{1,0:T(8,128)(2,1)S(1)}, bf16[784,128]{1,0:T(8,128)(2,1)S(1)}, u32[]{:S(2)}, u32[]{:S(2)}) collective-permute-start(bf16[784,128]{1,0:T(8,128)(2,1)S(1)} %get-tuple-element.40), channel_id=1, source_target_pairs={{0,192},{64,128},{128,64},{192,0},{1,193},{65,129},{129,65},{193,1... | collective-permute-start | bytes 602120 | tf_op jit(solution)/shard_map/ppermute | solution.py:23
  12.9 3.4 %collective-permute-start.1 = (bf16[1040,128]{1,0:T(8,128)(2,1)S(1)}, bf16[1040,128]{1,0:T(8,128)(2,1)S(1)}, u32[]{:S(2)}, u32[]{:S(2)}) collective-permute-start(bf16[1040,128]{1,0:T(8,128)(2,1)S(1)} %get-tuple-element.31), channel_id=1, source_target_pairs={{0,128},{64,192},{128,0},{192,64},{1,129},{65,193},{129,1},{193,65... | collective-permute-start | bytes 798728 | tf_op jit(solution)/shard_map/ppermute | solution.py:23
  16.3 1.5 %collective-permute-start.2 = (bf16[1040,128]{1,0:T(8,128)(2,1)S(1)}, bf16[1040,128]{1,0:T(8,128)(2,1)S(1)}, u32[]{:S(2)}, u32[]{:S(2)}) collective-permute-start(bf16[1040,128]{1,0:T(8,128)(2,1)S(1)} %get-tuple-element.32), channel_id=1, source_target_pairs={{0,192},{64,128},{128,64},{192,0},{1,193},{65,129},{129,65},{193,1... | collective-permute-start | bytes 798728 | tf_op jit(solution)/shard_map/ppermute | solution.py:23
  17.8 3.8 %collective-permute-done.9.refs_2_ = bf16[784,128]{1,0:T(8,128)(2,1)S(1)} collective-permute-done((bf16[784,128]{1,0:T(8,128)(2,1)S(1)}, bf16[784,128]{1,0:T(8,128)(2,1)S(1)}, u32[]{:S(2)}, u32[]{:S(2)}) %collective-permute-start.9) | collective-permute-done | bytes 200736 | tf_op jit(solution)/shard_map/ppermute | solution.py:23
  21.7 2.1 %collective-permute-start.20 = (bf16[4,528,128]{2,1,0:T(8,128)(2,1)S(1)}, bf16[4,528,128]{2,1,0:T(8,128)(2,1)S(1)}, u32[]{:S(2)}, u32[]{:S(2)}) collective-permute-start(bf16[4,528,128]{2,1,0:T(8,128)(2,1)S(1)} %pad_maximum_fusion.2.column), channel_id=1, source_target_pairs={{0,63},{1,2},{2,1},{3,4},{4,3},{5,6},{6,5},{7,8},{8,7},{9,10},{10,... | collective-permute-start | bytes 1622024 | tf_op jit(solution)/shard_map/ppermute | solution.py:23
  24.2 1.7 %collective-permute-done.refs_1_ = bf16[1040,128]{1,0:T(8,128)(2,1)S(1)} collective-permute-done((bf16[1040,128]{1,0:T(8,128)(2,1)S(1)}, bf16[1040,128]{1,0:T(8,128)(2,1)S(1)}, u32[]{:S(2)}, u32[]{:S(2)}) %collective-permute-start) | collective-permute-done | bytes 266272 | tf_op jit(solution)/shard_map/ppermute | solution.py:23
  25.9 4.3 %collective-permute-start.12 = (bf16[4,528,128]{2,1,0:T(8,128)(2,1)S(1)}, bf16[4,528,128]{2,1,0:T(8,128)(2,1)S(1)}, u32[]{:S(2)}, u32[]{:S(2)}) collective-permute-start(bf16[4,528,128]{2,1,0:T(8,128)(2,1)S(1)} %pad_maximum_fusion.1.column), channel_id=1, source_target_pairs={{0,63},{1,2},{2,1},{3,4},{4,3},{5,6},{6,5},{7,8},{8,7},{9,10},{10,... | collective-permute-start | bytes 1622024 | tf_op jit(solution)/shard_map/ppermute | solution.py:23
  30.3 1.9 %collective-permute-done.2.refs_3_ = bf16[1040,128]{1,0:T(8,128)(2,1)S(1)} collective-permute-done((bf16[1040,128]{1,0:T(8,128)(2,1)S(1)}, bf16[1040,128]{1,0:T(8,128)(2,1)S(1)}, u32[]{:S(2)}, u32[]{:S(2)}) %collective-permute-start.2) | collective-permute-done | bytes 266272 | tf_op jit(solution)/shard_map/ppermute | solution.py:23
  32.3 6.4 %collective-permute-start.4 = (bf16[4,528,128]{2,1,0:T(8,128)(2,1)S(1)}, bf16[4,528,128]{2,1,0:T(8,128)(2,1)S(1)}, u32[]{:S(2)}, u32[]{:S(2)}) collective-permute-start(bf16[4,528,128]{2,1,0:T(8,128)(2,1)S(1)} %pad_maximum_fusion.column), channel_id=1, source_target_pairs={{0,63},{1,2},{2,1},{3,4},{4,3},{5,6},{6,5},{7,8},{8,7},{9,10},{10,... | collective-permute-start | bytes 1622024 | tf_op jit(solution)/shard_map/ppermute | solution.py:23
  38.7 3.6 %attend.5 = (bf16[4,256,128]{2,1,0:T(8,128)(2,1)S(1)}, bf16[4,256,128]{2,1,0:T(8,128)(2,1)S(1)}, bf16[4,256,128]{2,1,0:T(8,128)(2,1)S(1)}, bf16[4,256,128]{2,1,0:T(8,128)(2,1)S(1)}) custom-call(s32[1,2]{1,0:T(1,128)S(1)} %copy-done, bf16[4,528,128]{2,1,0:T(8,128)(2,1)S(1)} %pad_maximum_fusion.2.column, ...), custom_call_target="tpu_custom_call" | custom-call | flops 1677721600 | bytes 2129920 | tf_op jit(solution)/shard_map/attend/pallas_call | solution.py:193
  42.7 4.3 %collective-permute-start.22 = (bf16[4,256,128]{2,1,0:T(8,128)(2,1)S(1)}, bf16[4,256,128]{2,1,0:T(8,128)(2,1)S(1)}, u32[]{:S(2)}, u32[]{:S(2)}) collective-permute-start(bf16[4,256,128]{2,1,0:T(8,128)(2,1)S(1)} %get-tuple-element.51), channel_id=1, source_target_pairs={{0,128},{64,192},{128,0},{192,64},{1,129},{65,193},{129,1},{193,65... | collective-permute-start | bytes 786440 | tf_op jit(solution)/shard_map/ppermute | solution.py:23
  47.3 3.6 %attend.4 = (bf16[4,256,128]{2,1,0:T(8,128)(2,1)S(1)}, bf16[4,256,128]{2,1,0:T(8,128)(2,1)S(1)}, bf16[4,256,128]{2,1,0:T(8,128)(2,1)S(1)}, bf16[4,256,128]{2,1,0:T(8,128)(2,1)S(1)}) custom-call(s32[1,2]{1,0:T(1,128)S(1)} %copy-done, bf16[4,528,128]{2,1,0:T(8,128)(2,1)S(1)} %pad_maximum_fusion.1.column, ...), custom_call_target="tpu_custom_call" | custom-call | flops 1677721600 | bytes 2129920 | tf_op jit(solution)/shard_map/attend/pallas_call | solution.py:193
  51.0 4.3 %collective-permute-start.14 = (bf16[4,256,128]{2,1,0:T(8,128)(2,1)S(1)}, bf16[4,256,128]{2,1,0:T(8,128)(2,1)S(1)}, u32[]{:S(2)}, u32[]{:S(2)}) collective-permute-start(bf16[4,256,128]{2,1,0:T(8,128)(2,1)S(1)} %get-tuple-element.43), channel_id=1, source_target_pairs={{0,128},{64,192},{128,0},{192,64},{1,129},{65,193},{129,1},{193,65... | collective-permute-start | bytes 786440 | tf_op jit(solution)/shard_map/ppermute | solution.py:23
  55.3 3.6 %attend.3 = (bf16[4,256,128]{2,1,0:T(8,128)(2,1)S(1)}, bf16[4,256,128]{2,1,0:T(8,128)(2,1)S(1)}, bf16[4,256,128]{2,1,0:T(8,128)(2,1)S(1)}, bf16[4,256,128]{2,1,0:T(8,128)(2,1)S(1)}) custom-call(s32[1,2]{1,0:T(1,128)S(1)} %copy-done, bf16[4,528,128]{2,1,0:T(8,128)(2,1)S(1)} %pad_maximum_fusion.column, bf16[4,528,128]{2,1,0:T(8,128)(2,1)S(1)} %collective-permute-done.3.near, ...), custom_call_target="tpu_custom_call" | custom-call | flops 1677721600 | bytes 2129920 | tf_op jit(solution)/shard_map/attend/pallas_call | solution.py:193
  59.0 0.4 collective-permute-start.15
  59.7 2.2 %collective-permute-done.23.refs_3_ = bf16[4,256,128]{2,1,0:T(8,128)(2,1)S(1)} collective-permute-done((bf16[4,256,128]{2,1,0:T(8,128)(2,1)S(1)}, bf16[4,256,128]{2,1,0:T(8,128)(2,1)S(1)}, u32[]{:S(2)}, u32[]{:S(2)}) %collective-permute-start.23) | collective-permute-done | bytes 262176 | tf_op jit(solution)/shard_map/ppermute | solution.py:23
  61.9 0.5 collective-permute-start.5
  62.4 0.6 collective-permute-done.13.refs_1_
  63.0 2.3 %collective-permute-start.6 = (bf16[4,256,128]{2,1,0:T(8,128)(2,1)S(1)}, bf16[4,256,128]{2,1,0:T(8,128)(2,1)S(1)}, u32[]{:S(2)}, u32[]{:S(2)}) collective-permute-start(bf16[4,256,128]{2,1,0:T(8,128)(2,1)S(1)} %get-tuple-element.34), channel_id=1, source_target_pairs={{0,128},{64,192},{128,0},{192,64},{1,129},{65,193},{129,1},{193,65... | collective-permute-start | bytes 786440 | tf_op jit(solution)/shard_map/ppermute | solution.py:23
  65.4 1.1 %put.4.refs_4_ = bf16[4,256,1536]{2,1,0:T(8,128)(2,1)} custom-call(bf16[4,256,128]{2,1,0:T(8,128)(2,1)S(1)} %get-tuple-element.49.refs_0_, bf16[4,256,128]{2,1,0:T(8,128)(2,1)S(1)} %collective-permute-done.21.refs_1_, bf16[4,256,128]{2,1,0:T(8,128)(2,1)S(1)} %collective-permute-done.22.refs_2_, bf16[4,256,128]{2,1,0:T(8,128)(2,1)S(1)} %collective-permute-done.23.refs_3_), custom_call_target="tpu_custom_call" | custom-call | bytes 2097152 | tf_op jit(solution)/shard_map/put/pallas_call | solution.py:247
  66.5 4.5 %collective-permute-done.14.refs_2_ = bf16[4,256,128]{2,1,0:T(8,128)(2,1)S(1)} collective-permute-done((bf16[4,256,128]{2,1,0:T(8,128)(2,1)S(1)}, bf16[4,256,128]{2,1,0:T(8,128)(2,1)S(1)}, u32[]{:S(2)}, u32[]{:S(2)}) %collective-permute-start.14) | collective-permute-done | bytes 262176 | tf_op jit(solution)/shard_map/ppermute | solution.py:23
  71.0 4.0 %collective-permute-done.15.refs_3_ = bf16[4,256,128]{2,1,0:T(8,128)(2,1)S(1)} collective-permute-done((bf16[4,256,128]{2,1,0:T(8,128)(2,1)S(1)}, bf16[4,256,128]{2,1,0:T(8,128)(2,1)S(1)}, u32[]{:S(2)}, u32[]{:S(2)}) %collective-permute-start.15) | collective-permute-done | bytes 262176 | tf_op jit(solution)/shard_map/ppermute | solution.py:23
  75.1 1.1 %put.5.refs_2_ = bf16[4,256,1536]{2,1,0:T(8,128)(2,1)} custom-call(bf16[4,256,128]{2,1,0:T(8,128)(2,1)S(1)} %get-tuple-element.41.refs_0_, bf16[4,256,128]{2,1,0:T(8,128)(2,1)S(1)} %collective-permute-done.13.refs_1_, bf16[4,256,128]{2,1,0:T(8,128)(2,1)S(1)} %collective-permute-done.14.refs_2_, ...), custom_call_target="tpu_custom_call", output_to_operand_aliasing={{}: (4, {})} | custom-call | bytes 2097152 | tf_op jit(solution)/shard_map/put/pallas_call | solution.py:247
  76.2 0.9 %put.6.refs_2_ = bf16[4,256,1536]{2,1,0:T(8,128)(2,1)} custom-call(bf16[4,256,128]{2,1,0:T(8,128)(2,1)S(1)} %get-tuple-element.35.refs_0_, bf16[4,256,128]{2,1,0:T(8,128)(2,1)S(1)} %collective-permute-done.7.refs_1_, bf16[4,256,1536]{2,1,0:T(8,128)(2,1)} %put.5.refs_2_), custom_call_target="tpu_custom_call", output_to_operand_aliasing={{}: (2, {})} | custom-call | bytes 1048576 | tf_op jit(solution)/shard_map/put/pallas_call | solution.py:247
  77.1 7.3 %collective-permute-done.5.refs_0_ = bf16[4,256,128]{2,1,0:T(8,128)(2,1)S(1)} collective-permute-done((bf16[4,256,128]{2,1,0:T(8,128)(2,1)S(1)}, bf16[4,256,128]{2,1,0:T(8,128)(2,1)S(1)}, u32[]{:S(2)}, u32[]{:S(2)}) %collective-permute-start.5) | collective-permute-done | bytes 262176 | tf_op jit(solution)/shard_map/ppermute | solution.py:23
  84.4 0.9 %put.7 = bf16[4,256,1536]{2,1,0:T(8,128)(2,1)} custom-call(bf16[4,256,128]{2,1,0:T(8,128)(2,1)S(1)} %collective-permute-done.5.refs_0_, bf16[4,256,128]{2,1,0:T(8,128)(2,1)S(1)} %collective-permute-done.6.refs_1_, bf16[4,256,1536]{2,1,0:T(8,128)(2,1)} %put.6.refs_2_), custom_call_target="tpu_custom_call", output_to_operand_aliasing={{}: (2, {})} | custom-call | bytes 1048576 | tf_op jit(solution)/shard_map/put/pallas_call | solution.py:247
  (38 shorter events, 1.9 us)
Async XLA Ops:
  1.2 10.2 %collective-permute-start.16 = (bf16[528,128]{1,0:T(8,128)(2,1)S(1)}, bf16[528,128]{1,0:T(8,128)(2,1)S(1)}, u32[]{:S(2)}, u32[]{:S(2)}) collective-permute-start(bf16[528,128]{1,0:T(8,128)(2,1)S(1)} %get-tuple-element.46), channel_id=1, source_target_pairs={{0,64},{64,0},{128,192},{192,128},{1,65},{65,1},{129,193},{193,129... | collective-permute-start | bytes 405512 | tf_op jit(solution)/shard_map/ppermute | solution.py:23
  2.1 10.8 %collective-permute-start.17 = (bf16[528,128]{1,0:T(8,128)(2,1)S(1)}, bf16[528,128]{1,0:T(8,128)(2,1)S(1)}, u32[]{:S(2)}, u32[]{:S(2)}) collective-permute-start(bf16[528,128]{1,0:T(8,128)(2,1)S(1)} %get-tuple-element.47), channel_id=1, source_target_pairs={{0,128},{64,192},{128,0},{192,64},{1,129},{65,193},{129,1},{193,65... | collective-permute-start | bytes 405512 | tf_op jit(solution)/shard_map/ppermute | solution.py:23
  4.7 8.2 %collective-permute-start.18 = (bf16[528,128]{1,0:T(8,128)(2,1)S(1)}, bf16[528,128]{1,0:T(8,128)(2,1)S(1)}, u32[]{:S(2)}, u32[]{:S(2)}) collective-permute-start(bf16[528,128]{1,0:T(8,128)(2,1)S(1)} %get-tuple-element.48), channel_id=1, source_target_pairs={{0,192},{64,128},{128,64},{192,0},{1,193},{65,129},{129,65},{193,1... | collective-permute-start | bytes 405512 | tf_op jit(solution)/shard_map/ppermute | solution.py:23
  7.9 30.7 %copy-start = (s32[1,2]{1,0:T(1,128)S(1)}, s32[1,2]{1,0:T(1,128)}, u32[]{:S(2)}) copy-start(s32[1,2]{1,0:T(1,128)} %lists.5) | copy-start | bytes 28
  7.9 8.4 %collective-permute-start.8 = (bf16[784,128]{1,0:T(8,128)(2,1)S(1)}, bf16[784,128]{1,0:T(8,128)(2,1)S(1)}, u32[]{:S(2)}, u32[]{:S(2)}) collective-permute-start(bf16[784,128]{1,0:T(8,128)(2,1)S(1)} %get-tuple-element.38), channel_id=1, source_target_pairs={{0,64},{64,0},{128,192},{192,128},{1,65},{65,1},{129,193},{193,129... | collective-permute-start | bytes 602120 | tf_op jit(solution)/shard_map/ppermute | solution.py:23
  8.0 13.6 %collective-permute-start.9 = (bf16[784,128]{1,0:T(8,128)(2,1)S(1)}, bf16[784,128]{1,0:T(8,128)(2,1)S(1)}, u32[]{:S(2)}, u32[]{:S(2)}) collective-permute-start(bf16[784,128]{1,0:T(8,128)(2,1)S(1)} %get-tuple-element.39), channel_id=1, source_target_pairs={{0,128},{64,192},{128,0},{192,64},{1,129},{65,193},{129,1},{193,65... | collective-permute-start | bytes 602120 | tf_op jit(solution)/shard_map/ppermute | solution.py:23
  11.5 12.6 %collective-permute-start.10 = (bf16[784,128]{1,0:T(8,128)(2,1)S(1)}, bf16[784,128]{1,0:T(8,128)(2,1)S(1)}, u32[]{:S(2)}, u32[]{:S(2)}) collective-permute-start(bf16[784,128]{1,0:T(8,128)(2,1)S(1)} %get-tuple-element.40), channel_id=1, source_target_pairs={{0,192},{64,128},{128,64},{192,0},{1,193},{65,129},{129,65},{193,1... | collective-permute-start | bytes 602120 | tf_op jit(solution)/shard_map/ppermute | solution.py:23
  12.9 13.0 %collective-permute-start = (bf16[1040,128]{1,0:T(8,128)(2,1)S(1)}, bf16[1040,128]{1,0:T(8,128)(2,1)S(1)}, u32[]{:S(2)}, u32[]{:S(2)}) collective-permute-start(bf16[1040,128]{1,0:T(8,128)(2,1)S(1)} %get-tuple-element.30), channel_id=1, source_target_pairs={{0,64},{64,0},{128,192},{192,128},{1,65},{65,1},{129,193},{193,129... | collective-permute-start | bytes 798728 | tf_op jit(solution)/shard_map/ppermute | solution.py:23
  12.9 17.3 %collective-permute-start.1 = (bf16[1040,128]{1,0:T(8,128)(2,1)S(1)}, bf16[1040,128]{1,0:T(8,128)(2,1)S(1)}, u32[]{:S(2)}, u32[]{:S(2)}) collective-permute-start(bf16[1040,128]{1,0:T(8,128)(2,1)S(1)} %get-tuple-element.31), channel_id=1, source_target_pairs={{0,128},{64,192},{128,0},{192,64},{1,129},{65,193},{129,1},{193,65... | collective-permute-start | bytes 798728 | tf_op jit(solution)/shard_map/ppermute | solution.py:23
  16.3 15.8 %collective-permute-start.2 = (bf16[1040,128]{1,0:T(8,128)(2,1)S(1)}, bf16[1040,128]{1,0:T(8,128)(2,1)S(1)}, u32[]{:S(2)}, u32[]{:S(2)}) collective-permute-start(bf16[1040,128]{1,0:T(8,128)(2,1)S(1)} %get-tuple-element.32), channel_id=1, source_target_pairs={{0,192},{64,128},{128,64},{192,0},{1,193},{65,129},{129,65},{193,1... | collective-permute-start | bytes 798728 | tf_op jit(solution)/shard_map/ppermute | solution.py:23
  21.7 17.0 %collective-permute-start.20 = (bf16[4,528,128]{2,1,0:T(8,128)(2,1)S(1)}, bf16[4,528,128]{2,1,0:T(8,128)(2,1)S(1)}, u32[]{:S(2)}, u32[]{:S(2)}) collective-permute-start(bf16[4,528,128]{2,1,0:T(8,128)(2,1)S(1)} %pad_maximum_fusion.2.column), channel_id=1, source_target_pairs={{0,63},{1,2},{2,1},{3,4},{4,3},{5,6},{6,5},{7,8},{8,7},{9,10},{10,... | collective-permute-start | bytes 1622024 | tf_op jit(solution)/shard_map/ppermute | solution.py:23
  24.1 14.6 %collective-permute-start.19 = (bf16[4,528,128]{2,1,0:T(8,128)(2,1)S(1)}, bf16[4,528,128]{2,1,0:T(8,128)(2,1)S(1)}, u32[]{:S(2)}, u32[]{:S(2)}) collective-permute-start(bf16[4,528,128]{2,1,0:T(8,128)(2,1)S(1)} %pad_maximum_fusion.2.column), channel_id=1, source_target_pairs={{0,1},{1,0},{2,3},{3,2},{4,5},{5,4},{6,7},{7,6},{8,9},{9,8},{10,11... | collective-permute-start | bytes 1622024 | tf_op jit(solution)/shard_map/ppermute | solution.py:23
  25.9 16.8 %collective-permute-start.12 = (bf16[4,528,128]{2,1,0:T(8,128)(2,1)S(1)}, bf16[4,528,128]{2,1,0:T(8,128)(2,1)S(1)}, u32[]{:S(2)}, u32[]{:S(2)}) collective-permute-start(bf16[4,528,128]{2,1,0:T(8,128)(2,1)S(1)} %pad_maximum_fusion.1.column), channel_id=1, source_target_pairs={{0,63},{1,2},{2,1},{3,4},{4,3},{5,6},{6,5},{7,8},{8,7},{9,10},{10,... | collective-permute-start | bytes 1622024 | tf_op jit(solution)/shard_map/ppermute | solution.py:23
  30.2 16.7 %collective-permute-start.11 = (bf16[4,528,128]{2,1,0:T(8,128)(2,1)S(1)}, bf16[4,528,128]{2,1,0:T(8,128)(2,1)S(1)}, u32[]{:S(2)}, u32[]{:S(2)}) collective-permute-start(bf16[4,528,128]{2,1,0:T(8,128)(2,1)S(1)} %pad_maximum_fusion.1.column), channel_id=1, source_target_pairs={{0,1},{1,0},{2,3},{3,2},{4,5},{5,4},{6,7},{7,6},{8,9},{9,8},{10,11... | collective-permute-start | bytes 1622024 | tf_op jit(solution)/shard_map/ppermute | solution.py:23
  32.3 18.6 %collective-permute-start.4 = (bf16[4,528,128]{2,1,0:T(8,128)(2,1)S(1)}, bf16[4,528,128]{2,1,0:T(8,128)(2,1)S(1)}, u32[]{:S(2)}, u32[]{:S(2)}) collective-permute-start(bf16[4,528,128]{2,1,0:T(8,128)(2,1)S(1)} %pad_maximum_fusion.column), channel_id=1, source_target_pairs={{0,63},{1,2},{2,1},{3,4},{4,3},{5,6},{6,5},{7,8},{8,7},{9,10},{10,... | collective-permute-start | bytes 1622024 | tf_op jit(solution)/shard_map/ppermute | solution.py:23
  38.7 12.3 %collective-permute-start.3 = (bf16[4,528,128]{2,1,0:T(8,128)(2,1)S(1)}, bf16[4,528,128]{2,1,0:T(8,128)(2,1)S(1)}, u32[]{:S(2)}, u32[]{:S(2)}) collective-permute-start(bf16[4,528,128]{2,1,0:T(8,128)(2,1)S(1)} %pad_maximum_fusion.column), channel_id=1, source_target_pairs={{0,1},{1,0},{2,3},{3,2},{4,5},{5,4},{6,7},{7,6},{8,9},{9,8},{10,11... | collective-permute-start | bytes 1622024 | tf_op jit(solution)/shard_map/ppermute | solution.py:23
  42.3 16.7 %collective-permute-start.21 = (bf16[4,256,128]{2,1,0:T(8,128)(2,1)S(1)}, bf16[4,256,128]{2,1,0:T(8,128)(2,1)S(1)}, u32[]{:S(2)}, u32[]{:S(2)}) collective-permute-start(bf16[4,256,128]{2,1,0:T(8,128)(2,1)S(1)} %get-tuple-element.50), channel_id=1, source_target_pairs={{0,64},{64,0},{128,192},{192,128},{1,65},{65,1},{129,193},{193,129... | collective-permute-start | bytes 786440 | tf_op jit(solution)/shard_map/ppermute | solution.py:23
  42.7 17.1 %collective-permute-start.22 = (bf16[4,256,128]{2,1,0:T(8,128)(2,1)S(1)}, bf16[4,256,128]{2,1,0:T(8,128)(2,1)S(1)}, u32[]{:S(2)}, u32[]{:S(2)}) collective-permute-start(bf16[4,256,128]{2,1,0:T(8,128)(2,1)S(1)} %get-tuple-element.51), channel_id=1, source_target_pairs={{0,128},{64,192},{128,0},{192,64},{1,129},{65,193},{129,1},{193,65... | collective-permute-start | bytes 786440 | tf_op jit(solution)/shard_map/ppermute | solution.py:23
  46.9 15.0 %collective-permute-start.23 = (bf16[4,256,128]{2,1,0:T(8,128)(2,1)S(1)}, bf16[4,256,128]{2,1,0:T(8,128)(2,1)S(1)}, u32[]{:S(2)}, u32[]{:S(2)}) collective-permute-start(bf16[4,256,128]{2,1,0:T(8,128)(2,1)S(1)} %get-tuple-element.52), channel_id=1, source_target_pairs={{0,192},{64,128},{128,64},{192,0},{1,193},{65,129},{129,65},{193,1... | collective-permute-start | bytes 786440 | tf_op jit(solution)/shard_map/ppermute | solution.py:23
  50.9 12.1 %collective-permute-start.13 = (bf16[4,256,128]{2,1,0:T(8,128)(2,1)S(1)}, bf16[4,256,128]{2,1,0:T(8,128)(2,1)S(1)}, u32[]{:S(2)}, u32[]{:S(2)}) collective-permute-start(bf16[4,256,128]{2,1,0:T(8,128)(2,1)S(1)} %get-tuple-element.42), channel_id=1, source_target_pairs={{0,64},{64,0},{128,192},{192,128},{1,65},{65,1},{129,193},{193,129... | collective-permute-start | bytes 786440 | tf_op jit(solution)/shard_map/ppermute | solution.py:23
  51.0 20.0 %collective-permute-start.14 = (bf16[4,256,128]{2,1,0:T(8,128)(2,1)S(1)}, bf16[4,256,128]{2,1,0:T(8,128)(2,1)S(1)}, u32[]{:S(2)}, u32[]{:S(2)}) collective-permute-start(bf16[4,256,128]{2,1,0:T(8,128)(2,1)S(1)} %get-tuple-element.43), channel_id=1, source_target_pairs={{0,128},{64,192},{128,0},{192,64},{1,129},{65,193},{129,1},{193,65... | collective-permute-start | bytes 786440 | tf_op jit(solution)/shard_map/ppermute | solution.py:23
  59.0 16.1 %collective-permute-start.15 = (bf16[4,256,128]{2,1,0:T(8,128)(2,1)S(1)}, bf16[4,256,128]{2,1,0:T(8,128)(2,1)S(1)}, u32[]{:S(2)}, u32[]{:S(2)}) collective-permute-start(bf16[4,256,128]{2,1,0:T(8,128)(2,1)S(1)} %get-tuple-element.44), channel_id=1, source_target_pairs={{0,192},{64,128},{128,64},{192,0},{1,193},{65,129},{129,65},{193,1... | collective-permute-start | bytes 786440 | tf_op jit(solution)/shard_map/ppermute | solution.py:23
  59.7 16.4 %collective-permute-start.7 = (bf16[4,256,128]{2,1,0:T(8,128)(2,1)S(1)}, bf16[4,256,128]{2,1,0:T(8,128)(2,1)S(1)}, u32[]{:S(2)}, u32[]{:S(2)}) collective-permute-start(bf16[4,256,128]{2,1,0:T(8,128)(2,1)S(1)} %get-tuple-element.36), channel_id=1, source_target_pairs={{0,64},{64,0},{128,192},{192,128},{1,65},{65,1},{129,193},{193,129... | collective-permute-start | bytes 786440 | tf_op jit(solution)/shard_map/ppermute | solution.py:23
  61.9 22.5 %collective-permute-start.5 = (bf16[4,256,128]{2,1,0:T(8,128)(2,1)S(1)}, bf16[4,256,128]{2,1,0:T(8,128)(2,1)S(1)}, u32[]{:S(2)}, u32[]{:S(2)}) collective-permute-start(bf16[4,256,128]{2,1,0:T(8,128)(2,1)S(1)} %get-tuple-element.33), channel_id=1, source_target_pairs={{0,192},{64,128},{128,64},{192,0},{1,193},{65,129},{129,65},{193,1... | collective-permute-start | bytes 786440 | tf_op jit(solution)/shard_map/ppermute | solution.py:23
  63.0 21.4 %collective-permute-start.6 = (bf16[4,256,128]{2,1,0:T(8,128)(2,1)S(1)}, bf16[4,256,128]{2,1,0:T(8,128)(2,1)S(1)}, u32[]{:S(2)}, u32[]{:S(2)}) collective-permute-start(bf16[4,256,128]{2,1,0:T(8,128)(2,1)S(1)} %get-tuple-element.34), channel_id=1, source_target_pairs={{0,128},{64,192},{128,0},{192,64},{1,129},{65,193},{129,1},{193,65... | collective-permute-start | bytes 786440 | tf_op jit(solution)/shard_map/ppermute | solution.py:23

commit v2 on v1

--- a/solution.py
+++ b/solution.py
@@ -222,19 +222,14 @@
 
 def put_body(*refs, slots, per_dev, chunk, dim):
     pieces = refs[: len(slots)]
-    out, buf, in_sem, out_sem = refs[-4:]
+    out, sem = refs[-2:]
     me = lax.axis_index("tm")
-    loads = []
     stores = []
     for n, i in enumerate(slots):
         where = pl.ds(pl.multiple_of(((me ^ i) * per_dev + chunk) * dim, dim), dim)
-        loads.append(pltpu.make_async_copy(pieces[n], buf.at[n], in_sem.at[n]))
-        stores.append(pltpu.make_async_copy(buf.at[n], out.at[:, :, where], out_sem.at[n]))
-    for copy in loads:
+        stores.append(pltpu.make_async_copy(pieces[n], out.at[:, :, where], sem.at[n]))
+    for copy in stores:
         copy.start()
-    for load, store in zip(loads, stores):
-        load.wait()
-        store.start()
     for copy in stores:
         copy.wait()
 
@@ -243,16 +238,13 @@
     pieces = [pieces[i] for i in slots]
     peers = len(pieces)
     _, _, dim = pieces[0].shape
-    args = list(pieces) if prior is None else list(pieces) + [prior]
+    args = pieces if prior is None else pieces + [prior]
+    inside = pl.BlockSpec(memory_space=pltpu.VMEM)
     return pl.pallas_call(
         functools.partial(put_body, slots=slots, per_dev=per_dev, chunk=chunk, dim=dim),
-        in_specs=[ANY] * len(args),
+        in_specs=[inside] * peers + [ANY] * (len(args) - peers),
         out_specs=ANY,
-        scratch_shapes=[
-            pltpu.VMEM((peers,) + pieces[0].shape, BF16),
-            pltpu.SemaphoreType.DMA((peers,)),
-            pltpu.SemaphoreType.DMA((peers,)),
-        ],
+        scratch_shapes=[pltpu.SemaphoreType.DMA((peers,))],
         out_shape=jax.ShapeDtypeStruct(shape, BF16),
         input_output_aliases={} if prior is None else {peers: 0},
         compiler_params=pltpu.CompilerParams(vmem_limit_bytes=LIMIT),

time: 85.6 us -> 85.6 us (level)
  transfers between devices with their start and end apart: 24 -> 24, of which waited for: 10 -> 10; matrix products, arithmetic and copies ran while one was open for 0% -> 0% of each run, Pallas kernels for 19% -> 18%
where the time goes in v2:
time: 85.6 us; the launch traced here: 85.4 us
  starting transfers between devices  40.1 us (47%)
  waiting for transfers between devices  27 us (32%)
  Pallas kernels  17.6 us (21%)
    ppermute x24, starting transfers between devices, paired(): lax.ppermute(x, axis, [(i, mate(i)) for i in range(lax.axis_size(axis))])  40.1 us
    ppermute x24, waiting for transfers between devices, paired(): lax.ppermute(x, axis, [(i, mate(i)) for i in range(lax.axis_size(axis))])  27 us
    pallas_call x3, Pallas kernels, attend(): pl.pallas_call(functools.partial(attend_body, slots=slots, ask_at=ask_at,...  10.8 us
    pallas_call x4, Pallas kernels, put(): pl.pallas_call(functools.partial(put_body, slots=slots, per_dev=per_dev,...  3.62 us
    pallas_call x2, Pallas kernels, pack(): pl.pallas_call(functools.partial(pack_body, peers=peers, per_dev=per_dev,...  3.12 us
  transfers between devices with their start and end apart: 24, of which 10 were waited for; matrix products, arithmetic and copies ran while one was open for 0% of the time, Pallas kernels for 18%

profile of v2, /device:TPU:24, one launch (start us, length us, event | category | flops | bytes accessed | tf_op | source)
XLA Modules:
  0.0 85.4 jit_solution(2221676451797811412)
XLA Ops:
  0.0 1.2 %pack.3 = (bf16[528,128]{1,0:T(8,128)(2,1)S(1)}, bf16[528,128]{1,0:T(8,128)(2,1)S(1)}, bf16[528,128]{1,0:T(8,128)(2,1)S(1)}, bf16[528,128]{1,0:T(8,128)(2,1)S(1)}) custom-call(bf16[256,1536]{1,0:T(8,128)(2,1)} %bitcast.26, bf16[256,1536]{1,0:T(8,128)(2,1)} %bitcast.28, bf16[256,1536]{1,0:T(8,128)(2,1)} %bitcast.30, s32[4,12,4,64]{3,2,1,0:T(4,128)} %bitcast.32), custom_call_target="tpu_custom_call" | custom-call | bytes 1081344 | tf_op jit(solution)/shard_map/pack/pallas_call | solution.py:68
  1.2 0.8 collective-permute-start.16
  2.1 2.6 %collective-permute-start.17 = (bf16[528,128]{1,0:T(8,128)(2,1)S(1)}, bf16[528,128]{1,0:T(8,128)(2,1)S(1)}, u32[]{:S(2)}, u32[]{:S(2)}) collective-permute-start(bf16[528,128]{1,0:T(8,128)(2,1)S(1)} %get-tuple-element.47), channel_id=1, source_target_pairs={{0,128},{64,192},{128,0},{192,64},{1,129},{65,193},{129,1},{193,65... | collective-permute-start | bytes 405512 | tf_op jit(solution)/shard_map/ppermute | solution.py:23
  4.7 1.3 %collective-permute-start.18 = (bf16[528,128]{1,0:T(8,128)(2,1)S(1)}, bf16[528,128]{1,0:T(8,128)(2,1)S(1)}, u32[]{:S(2)}, u32[]{:S(2)}) collective-permute-start(bf16[528,128]{1,0:T(8,128)(2,1)S(1)} %get-tuple-element.48), channel_id=1, source_target_pairs={{0,192},{64,128},{128,64},{192,0},{1,193},{65,129},{129,65},{193,1... | collective-permute-start | bytes 405512 | tf_op jit(solution)/shard_map/ppermute | solution.py:23
  6.0 1.9 %pack.2 = (bf16[784,128]{1,0:T(8,128)(2,1)S(1)}, bf16[784,128]{1,0:T(8,128)(2,1)S(1)}, bf16[784,128]{1,0:T(8,128)(2,1)S(1)}, bf16[784,128]{1,0:T(8,128)(2,1)S(1)...) custom-call(bf16[256,1536]{1,0:T(8,128)(2,1)} %bitcast.27, ...), custom_call_target="tpu_custom_call" | custom-call | bytes 3735552 | tf_op jit(solution)/shard_map/pack/pallas_call | solution.py:68
  8.0 3.4 %collective-permute-start.9 = (bf16[784,128]{1,0:T(8,128)(2,1)S(1)}, bf16[784,128]{1,0:T(8,128)(2,1)S(1)}, u32[]{:S(2)}, u32[]{:S(2)}) collective-permute-start(bf16[784,128]{1,0:T(8,128)(2,1)S(1)} %get-tuple-element.39), channel_id=1, source_target_pairs={{0,128},{64,192},{128,0},{192,64},{1,129},{65,193},{129,1},{193,65... | collective-permute-start | bytes 602120 | tf_op jit(solution)/shard_map/ppermute | solution.py:23
  11.5 1.4 %collective-permute-start.10 = (bf16[784,128]{1,0:T(8,128)(2,1)S(1)}, bf16[784,128]{1,0:T(8,128)(2,1)S(1)}, u32[]{:S(2)}, u32[]{:S(2)}) collective-permute-start(bf16[784,128]{1,0:T(8,128)(2,1)S(1)} %get-tuple-element.40), channel_id=1, source_target_pairs={{0,192},{64,128},{128,64},{192,0},{1,193},{65,129},{129,65},{193,1... | collective-permute-start | bytes 602120 | tf_op jit(solution)/shard_map/ppermute | solution.py:23
  12.9 3.4 %collective-permute-start.1 = (bf16[1040,128]{1,0:T(8,128)(2,1)S(1)}, bf16[1040,128]{1,0:T(8,128)(2,1)S(1)}, u32[]{:S(2)}, u32[]{:S(2)}) collective-permute-start(bf16[1040,128]{1,0:T(8,128)(2,1)S(1)} %get-tuple-element.31), channel_id=1, source_target_pairs={{0,128},{64,192},{128,0},{192,64},{1,129},{65,193},{129,1},{193,65... | collective-permute-start | bytes 798728 | tf_op jit(solution)/shard_map/ppermute | solution.py:23
  16.3 1.5 %collective-permute-start.2 = (bf16[1040,128]{1,0:T(8,128)(2,1)S(1)}, bf16[1040,128]{1,0:T(8,128)(2,1)S(1)}, u32[]{:S(2)}, u32[]{:S(2)}) collective-permute-start(bf16[1040,128]{1,0:T(8,128)(2,1)S(1)} %get-tuple-element.32), channel_id=1, source_target_pairs={{0,192},{64,128},{128,64},{192,0},{1,193},{65,129},{129,65},{193,1... | collective-permute-start | bytes 798728 | tf_op jit(solution)/shard_map/ppermute | solution.py:23
  17.8 3.8 %collective-permute-done.9.refs_2_ = bf16[784,128]{1,0:T(8,128)(2,1)S(1)} collective-permute-done((bf16[784,128]{1,0:T(8,128)(2,1)S(1)}, bf16[784,128]{1,0:T(8,128)(2,1)S(1)}, u32[]{:S(2)}, u32[]{:S(2)}) %collective-permute-start.9) | collective-permute-done | bytes 200736 | tf_op jit(solution)/shard_map/ppermute | solution.py:23
  21.7 2.1 %collective-permute-start.20 = (bf16[4,528,128]{2,1,0:T(8,128)(2,1)S(1)}, bf16[4,528,128]{2,1,0:T(8,128)(2,1)S(1)}, u32[]{:S(2)}, u32[]{:S(2)}) collective-permute-start(bf16[4,528,128]{2,1,0:T(8,128)(2,1)S(1)} %pad_maximum_fusion.2.column), channel_id=1, source_target_pairs={{0,63},{1,2},{2,1},{3,4},{4,3},{5,6},{6,5},{7,8},{8,7},{9,10},{10,... | collective-permute-start | bytes 1622024 | tf_op jit(solution)/shard_map/ppermute | solution.py:23
  24.2 1.7 %collective-permute-done.refs_1_ = bf16[1040,128]{1,0:T(8,128)(2,1)S(1)} collective-permute-done((bf16[1040,128]{1,0:T(8,128)(2,1)S(1)}, bf16[1040,128]{1,0:T(8,128)(2,1)S(1)}, u32[]{:S(2)}, u32[]{:S(2)}) %collective-permute-start) | collective-permute-done | bytes 266272 | tf_op jit(solution)/shard_map/ppermute | solution.py:23
  25.9 4.3 %collective-permute-start.12 = (bf16[4,528,128]{2,1,0:T(8,128)(2,1)S(1)}, bf16[4,528,128]{2,1,0:T(8,128)(2,1)S(1)}, u32[]{:S(2)}, u32[]{:S(2)}) collective-permute-start(bf16[4,528,128]{2,1,0:T(8,128)(2,1)S(1)} %pad_maximum_fusion.1.column), channel_id=1, source_target_pairs={{0,63},{1,2},{2,1},{3,4},{4,3},{5,6},{6,5},{7,8},{8,7},{9,10},{10,... | collective-permute-start | bytes 1622024 | tf_op jit(solution)/shard_map/ppermute | solution.py:23
  30.3 1.9 %collective-permute-done.2.refs_3_ = bf16[1040,128]{1,0:T(8,128)(2,1)S(1)} collective-permute-done((bf16[1040,128]{1,0:T(8,128)(2,1)S(1)}, bf16[1040,128]{1,0:T(8,128)(2,1)S(1)}, u32[]{:S(2)}, u32[]{:S(2)}) %collective-permute-start.2) | collective-permute-done | bytes 266272 | tf_op jit(solution)/shard_map/ppermute | solution.py:23
  32.3 6.4 %collective-permute-start.4 = (bf16[4,528,128]{2,1,0:T(8,128)(2,1)S(1)}, bf16[4,528,128]{2,1,0:T(8,128)(2,1)S(1)}, u32[]{:S(2)}, u32[]{:S(2)}) collective-permute-start(bf16[4,528,128]{2,1,0:T(8,128)(2,1)S(1)} %pad_maximum_fusion.column), channel_id=1, source_target_pairs={{0,63},{1,2},{2,1},{3,4},{4,3},{5,6},{6,5},{7,8},{8,7},{9,10},{10,... | collective-permute-start | bytes 1622024 | tf_op jit(solution)/shard_map/ppermute | solution.py:23
  38.7 3.6 %attend.5 = (bf16[4,256,128]{2,1,0:T(8,128)(2,1)S(1)}, bf16[4,256,128]{2,1,0:T(8,128)(2,1)S(1)}, bf16[4,256,128]{2,1,0:T(8,128)(2,1)S(1)}, bf16[4,256,128]{2,1,0:T(8,128)(2,1)S(1)}) custom-call(s32[1,2]{1,0:T(1,128)S(1)} %copy-done, bf16[4,528,128]{2,1,0:T(8,128)(2,1)S(1)} %pad_maximum_fusion.2.column, ...), custom_call_target="tpu_custom_call" | custom-call | flops 1677721600 | bytes 2129920 | tf_op jit(solution)/shard_map/attend/pallas_call | solution.py:193
  42.7 4.3 %collective-permute-start.22 = (bf16[4,256,128]{2,1,0:T(8,128)(2,1)S(1)}, bf16[4,256,128]{2,1,0:T(8,128)(2,1)S(1)}, u32[]{:S(2)}, u32[]{:S(2)}) collective-permute-start(bf16[4,256,128]{2,1,0:T(8,128)(2,1)S(1)} %get-tuple-element.51), channel_id=1, source_target_pairs={{0,128},{64,192},{128,0},{192,64},{1,129},{65,193},{129,1},{193,65... | collective-permute-start | bytes 786440 | tf_op jit(solution)/shard_map/ppermute | solution.py:23
  47.3 3.6 %attend.4 = (bf16[4,256,128]{2,1,0:T(8,128)(2,1)S(1)}, bf16[4,256,128]{2,1,0:T(8,128)(2,1)S(1)}, bf16[4,256,128]{2,1,0:T(8,128)(2,1)S(1)}, bf16[4,256,128]{2,1,0:T(8,128)(2,1)S(1)}) custom-call(s32[1,2]{1,0:T(1,128)S(1)} %copy-done, bf16[4,528,128]{2,1,0:T(8,128)(2,1)S(1)} %pad_maximum_fusion.1.column, ...), custom_call_target="tpu_custom_call" | custom-call | flops 1677721600 | bytes 2129920 | tf_op jit(solution)/shard_map/attend/pallas_call | solution.py:193
  51.0 4.3 %collective-permute-start.14 = (bf16[4,256,128]{2,1,0:T(8,128)(2,1)S(1)}, bf16[4,256,128]{2,1,0:T(8,128)(2,1)S(1)}, u32[]{:S(2)}, u32[]{:S(2)}) collective-permute-start(bf16[4,256,128]{2,1,0:T(8,128)(2,1)S(1)} %get-tuple-element.43), channel_id=1, source_target_pairs={{0,128},{64,192},{128,0},{192,64},{1,129},{65,193},{129,1},{193,65... | collective-permute-start | bytes 786440 | tf_op jit(solution)/shard_map/ppermute | solution.py:23
  55.3 3.6 %attend.3 = (bf16[4,256,128]{2,1,0:T(8,128)(2,1)S(1)}, bf16[4,256,128]{2,1,0:T(8,128)(2,1)S(1)}, bf16[4,256,128]{2,1,0:T(8,128)(2,1)S(1)}, bf16[4,256,128]{2,1,0:T(8,128)(2,1)S(1)}) custom-call(s32[1,2]{1,0:T(1,128)S(1)} %copy-done, bf16[4,528,128]{2,1,0:T(8,128)(2,1)S(1)} %pad_maximum_fusion.column, bf16[4,528,128]{2,1,0:T(8,128)(2,1)S(1)} %collective-permute-done.3.near, ...), custom_call_target="tpu_custom_call" | custom-call | flops 1677721600 | bytes 2129920 | tf_op jit(solution)/shard_map/attend/pallas_call | solution.py:193
  59.0 0.4 collective-permute-start.15
  59.7 2.2 %collective-permute-done.23.refs_3_ = bf16[4,256,128]{2,1,0:T(8,128)(2,1)S(1)} collective-permute-done((bf16[4,256,128]{2,1,0:T(8,128)(2,1)S(1)}, bf16[4,256,128]{2,1,0:T(8,128)(2,1)S(1)}, u32[]{:S(2)}, u32[]{:S(2)}) %collective-permute-start.23) | collective-permute-done | bytes 262176 | tf_op jit(solution)/shard_map/ppermute | solution.py:23
  61.9 0.5 collective-permute-start.5
  62.4 0.6 collective-permute-done.13.refs_1_
  63.0 2.3 %collective-permute-start.6 = (bf16[4,256,128]{2,1,0:T(8,128)(2,1)S(1)}, bf16[4,256,128]{2,1,0:T(8,128)(2,1)S(1)}, u32[]{:S(2)}, u32[]{:S(2)}) collective-permute-start(bf16[4,256,128]{2,1,0:T(8,128)(2,1)S(1)} %get-tuple-element.34), channel_id=1, source_target_pairs={{0,128},{64,192},{128,0},{192,64},{1,129},{65,193},{129,1},{193,65... | collective-permute-start | bytes 786440 | tf_op jit(solution)/shard_map/ppermute | solution.py:23
  65.4 1.0 %put.4.refs_4_ = bf16[4,256,1536]{2,1,0:T(8,128)(2,1)} custom-call(bf16[4,256,128]{2,1,0:T(8,128)(2,1)S(1)} %get-tuple-element.49.refs_0_, bf16[4,256,128]{2,1,0:T(8,128)(2,1)S(1)} %collective-permute-done.21.refs_1_, bf16[4,256,128]{2,1,0:T(8,128)(2,1)S(1)} %collective-permute-done.22.refs_2_, bf16[4,256,128]{2,1,0:T(8,128)(2,1)S(1)} %collective-permute-done.23.refs_3_), custom_call_target="tpu_custom_call" | custom-call | bytes 2097152 | tf_op jit(solution)/shard_map/put/pallas_call | solution.py:243
  66.4 4.7 %collective-permute-done.14.refs_2_ = bf16[4,256,128]{2,1,0:T(8,128)(2,1)S(1)} collective-permute-done((bf16[4,256,128]{2,1,0:T(8,128)(2,1)S(1)}, bf16[4,256,128]{2,1,0:T(8,128)(2,1)S(1)}, u32[]{:S(2)}, u32[]{:S(2)}) %collective-permute-start.14) | collective-permute-done | bytes 262176 | tf_op jit(solution)/shard_map/ppermute | solution.py:23
  71.0 4.0 %collective-permute-done.15.refs_3_ = bf16[4,256,128]{2,1,0:T(8,128)(2,1)S(1)} collective-permute-done((bf16[4,256,128]{2,1,0:T(8,128)(2,1)S(1)}, bf16[4,256,128]{2,1,0:T(8,128)(2,1)S(1)}, u32[]{:S(2)}, u32[]{:S(2)}) %collective-permute-start.15) | collective-permute-done | bytes 262176 | tf_op jit(solution)/shard_map/ppermute | solution.py:23
  75.1 1.0 %put.5.refs_2_ = bf16[4,256,1536]{2,1,0:T(8,128)(2,1)} custom-call(bf16[4,256,128]{2,1,0:T(8,128)(2,1)S(1)} %get-tuple-element.41.refs_0_, bf16[4,256,128]{2,1,0:T(8,128)(2,1)S(1)} %collective-permute-done.13.refs_1_, bf16[4,256,128]{2,1,0:T(8,128)(2,1)S(1)} %collective-permute-done.14.refs_2_, ...), custom_call_target="tpu_custom_call", output_to_operand_aliasing={{}: (4, {})} | custom-call | bytes 2097152 | tf_op jit(solution)/shard_map/put/pallas_call | solution.py:243
  76.1 0.8 put.6.refs_2_
  76.9 7.5 %collective-permute-done.5.refs_0_ = bf16[4,256,128]{2,1,0:T(8,128)(2,1)S(1)} collective-permute-done((bf16[4,256,128]{2,1,0:T(8,128)(2,1)S(1)}, bf16[4,256,128]{2,1,0:T(8,128)(2,1)S(1)}, u32[]{:S(2)}, u32[]{:S(2)}) %collective-permute-start.5) | collective-permute-done | bytes 262176 | tf_op jit(solution)/shard_map/ppermute | solution.py:23
  84.4 0.8 put.7
  (38 shorter events, 1.9 us)
Async XLA Ops:
  1.2 10.2 %collective-permute-start.16 = (bf16[528,128]{1,0:T(8,128)(2,1)S(1)}, bf16[528,128]{1,0:T(8,128)(2,1)S(1)}, u32[]{:S(2)}, u32[]{:S(2)}) collective-permute-start(bf16[528,128]{1,0:T(8,128)(2,1)S(1)} %get-tuple-element.46), channel_id=1, source_target_pairs={{0,64},{64,0},{128,192},{192,128},{1,65},{65,1},{129,193},{193,129... | collective-permute-start | bytes 405512 | tf_op jit(solution)/shard_map/ppermute | solution.py:23
  2.1 10.8 %collective-permute-start.17 = (bf16[528,128]{1,0:T(8,128)(2,1)S(1)}, bf16[528,128]{1,0:T(8,128)(2,1)S(1)}, u32[]{:S(2)}, u32[]{:S(2)}) collective-permute-start(bf16[528,128]{1,0:T(8,128)(2,1)S(1)} %get-tuple-element.47), channel_id=1, source_target_pairs={{0,128},{64,192},{128,0},{192,64},{1,129},{65,193},{129,1},{193,65... | collective-permute-start | bytes 405512 | tf_op jit(solution)/shard_map/ppermute | solution.py:23
  4.7 8.2 %collective-permute-start.18 = (bf16[528,128]{1,0:T(8,128)(2,1)S(1)}, bf16[528,128]{1,0:T(8,128)(2,1)S(1)}, u32[]{:S(2)}, u32[]{:S(2)}) collective-permute-start(bf16[528,128]{1,0:T(8,128)(2,1)S(1)} %get-tuple-element.48), channel_id=1, source_target_pairs={{0,192},{64,128},{128,64},{192,0},{1,193},{65,129},{129,65},{193,1... | collective-permute-start | bytes 405512 | tf_op jit(solution)/shard_map/ppermute | solution.py:23
  7.9 30.7 %copy-start = (s32[1,2]{1,0:T(1,128)S(1)}, s32[1,2]{1,0:T(1,128)}, u32[]{:S(2)}) copy-start(s32[1,2]{1,0:T(1,128)} %lists.5) | copy-start | bytes 28
  7.9 8.4 %collective-permute-start.8 = (bf16[784,128]{1,0:T(8,128)(2,1)S(1)}, bf16[784,128]{1,0:T(8,128)(2,1)S(1)}, u32[]{:S(2)}, u32[]{:S(2)}) collective-permute-start(bf16[784,128]{1,0:T(8,128)(2,1)S(1)} %get-tuple-element.38), channel_id=1, source_target_pairs={{0,64},{64,0},{128,192},{192,128},{1,65},{65,1},{129,193},{193,129... | collective-permute-start | bytes 602120 | tf_op jit(solution)/shard_map/ppermute | solution.py:23
  8.0 13.6 %collective-permute-start.9 = (bf16[784,128]{1,0:T(8,128)(2,1)S(1)}, bf16[784,128]{1,0:T(8,128)(2,1)S(1)}, u32[]{:S(2)}, u32[]{:S(2)}) collective-permute-start(bf16[784,128]{1,0:T(8,128)(2,1)S(1)} %get-tuple-element.39), channel_id=1, source_target_pairs={{0,128},{64,192},{128,0},{192,64},{1,129},{65,193},{129,1},{193,65... | collective-permute-start | bytes 602120 | tf_op jit(solution)/shard_map/ppermute | solution.py:23
  11.5 12.6 %collective-permute-start.10 = (bf16[784,128]{1,0:T(8,128)(2,1)S(1)}, bf16[784,128]{1,0:T(8,128)(2,1)S(1)}, u32[]{:S(2)}, u32[]{:S(2)}) collective-permute-start(bf16[784,128]{1,0:T(8,128)(2,1)S(1)} %get-tuple-element.40), channel_id=1, source_target_pairs={{0,192},{64,128},{128,64},{192,0},{1,193},{65,129},{129,65},{193,1... | collective-permute-start | bytes 602120 | tf_op jit(solution)/shard_map/ppermute | solution.py:23
  12.9 13.0 %collective-permute-start = (bf16[1040,128]{1,0:T(8,128)(2,1)S(1)}, bf16[1040,128]{1,0:T(8,128)(2,1)S(1)}, u32[]{:S(2)}, u32[]{:S(2)}) collective-permute-start(bf16[1040,128]{1,0:T(8,128)(2,1)S(1)} %get-tuple-element.30), channel_id=1, source_target_pairs={{0,64},{64,0},{128,192},{192,128},{1,65},{65,1},{129,193},{193,129... | collective-permute-start | bytes 798728 | tf_op jit(solution)/shard_map/ppermute | solution.py:23
  12.9 17.3 %collective-permute-start.1 = (bf16[1040,128]{1,0:T(8,128)(2,1)S(1)}, bf16[1040,128]{1,0:T(8,128)(2,1)S(1)}, u32[]{:S(2)}, u32[]{:S(2)}) collective-permute-start(bf16[1040,128]{1,0:T(8,128)(2,1)S(1)} %get-tuple-element.31), channel_id=1, source_target_pairs={{0,128},{64,192},{128,0},{192,64},{1,129},{65,193},{129,1},{193,65... | collective-permute-start | bytes 798728 | tf_op jit(solution)/shard_map/ppermute | solution.py:23
  16.3 15.8 %collective-permute-start.2 = (bf16[1040,128]{1,0:T(8,128)(2,1)S(1)}, bf16[1040,128]{1,0:T(8,128)(2,1)S(1)}, u32[]{:S(2)}, u32[]{:S(2)}) collective-permute-start(bf16[1040,128]{1,0:T(8,128)(2,1)S(1)} %get-tuple-element.32), channel_id=1, source_target_pairs={{0,192},{64,128},{128,64},{192,0},{1,193},{65,129},{129,65},{193,1... | collective-permute-start | bytes 798728 | tf_op jit(solution)/shard_map/ppermute | solution.py:23
  21.7 17.0 %collective-permute-start.20 = (bf16[4,528,128]{2,1,0:T(8,128)(2,1)S(1)}, bf16[4,528,128]{2,1,0:T(8,128)(2,1)S(1)}, u32[]{:S(2)}, u32[]{:S(2)}) collective-permute-start(bf16[4,528,128]{2,1,0:T(8,128)(2,1)S(1)} %pad_maximum_fusion.2.column), channel_id=1, source_target_pairs={{0,63},{1,2},{2,1},{3,4},{4,3},{5,6},{6,5},{7,8},{8,7},{9,10},{10,... | collective-permute-start | bytes 1622024 | tf_op jit(solution)/shard_map/ppermute | solution.py:23
  24.1 14.6 %collective-permute-start.19 = (bf16[4,528,128]{2,1,0:T(8,128)(2,1)S(1)}, bf16[4,528,128]{2,1,0:T(8,128)(2,1)S(1)}, u32[]{:S(2)}, u32[]{:S(2)}) collective-permute-start(bf16[4,528,128]{2,1,0:T(8,128)(2,1)S(1)} %pad_maximum_fusion.2.column), channel_id=1, source_target_pairs={{0,1},{1,0},{2,3},{3,2},{4,5},{5,4},{6,7},{7,6},{8,9},{9,8},{10,11... | collective-permute-start | bytes 1622024 | tf_op jit(solution)/shard_map/ppermute | solution.py:23
  25.9 16.8 %collective-permute-start.12 = (bf16[4,528,128]{2,1,0:T(8,128)(2,1)S(1)}, bf16[4,528,128]{2,1,0:T(8,128)(2,1)S(1)}, u32[]{:S(2)}, u32[]{:S(2)}) collective-permute-start(bf16[4,528,128]{2,1,0:T(8,128)(2,1)S(1)} %pad_maximum_fusion.1.column), channel_id=1, source_target_pairs={{0,63},{1,2},{2,1},{3,4},{4,3},{5,6},{6,5},{7,8},{8,7},{9,10},{10,... | collective-permute-start | bytes 1622024 | tf_op jit(solution)/shard_map/ppermute | solution.py:23
  30.2 16.7 %collective-permute-start.11 = (bf16[4,528,128]{2,1,0:T(8,128)(2,1)S(1)}, bf16[4,528,128]{2,1,0:T(8,128)(2,1)S(1)}, u32[]{:S(2)}, u32[]{:S(2)}) collective-permute-start(bf16[4,528,128]{2,1,0:T(8,128)(2,1)S(1)} %pad_maximum_fusion.1.column), channel_id=1, source_target_pairs={{0,1},{1,0},{2,3},{3,2},{4,5},{5,4},{6,7},{7,6},{8,9},{9,8},{10,11... | collective-permute-start | bytes 1622024 | tf_op jit(solution)/shard_map/ppermute | solution.py:23
  32.3 18.6 %collective-permute-start.4 = (bf16[4,528,128]{2,1,0:T(8,128)(2,1)S(1)}, bf16[4,528,128]{2,1,0:T(8,128)(2,1)S(1)}, u32[]{:S(2)}, u32[]{:S(2)}) collective-permute-start(bf16[4,528,128]{2,1,0:T(8,128)(2,1)S(1)} %pad_maximum_fusion.column), channel_id=1, source_target_pairs={{0,63},{1,2},{2,1},{3,4},{4,3},{5,6},{6,5},{7,8},{8,7},{9,10},{10,... | collective-permute-start | bytes 1622024 | tf_op jit(solution)/shard_map/ppermute | solution.py:23
  38.7 12.3 %collective-permute-start.3 = (bf16[4,528,128]{2,1,0:T(8,128)(2,1)S(1)}, bf16[4,528,128]{2,1,0:T(8,128)(2,1)S(1)}, u32[]{:S(2)}, u32[]{:S(2)}) collective-permute-start(bf16[4,528,128]{2,1,0:T(8,128)(2,1)S(1)} %pad_maximum_fusion.column), channel_id=1, source_target_pairs={{0,1},{1,0},{2,3},{3,2},{4,5},{5,4},{6,7},{7,6},{8,9},{9,8},{10,11... | collective-permute-start | bytes 1622024 | tf_op jit(solution)/shard_map/ppermute | solution.py:23
  42.3 16.7 %collective-permute-start.21 = (bf16[4,256,128]{2,1,0:T(8,128)(2,1)S(1)}, bf16[4,256,128]{2,1,0:T(8,128)(2,1)S(1)}, u32[]{:S(2)}, u32[]{:S(2)}) collective-permute-start(bf16[4,256,128]{2,1,0:T(8,128)(2,1)S(1)} %get-tuple-element.50), channel_id=1, source_target_pairs={{0,64},{64,0},{128,192},{192,128},{1,65},{65,1},{129,193},{193,129... | collective-permute-start | bytes 786440 | tf_op jit(solution)/shard_map/ppermute | solution.py:23
  42.7 17.1 %collective-permute-start.22 = (bf16[4,256,128]{2,1,0:T(8,128)(2,1)S(1)}, bf16[4,256,128]{2,1,0:T(8,128)(2,1)S(1)}, u32[]{:S(2)}, u32[]{:S(2)}) collective-permute-start(bf16[4,256,128]{2,1,0:T(8,128)(2,1)S(1)} %get-tuple-element.51), channel_id=1, source_target_pairs={{0,128},{64,192},{128,0},{192,64},{1,129},{65,193},{129,1},{193,65... | collective-permute-start | bytes 786440 | tf_op jit(solution)/shard_map/ppermute | solution.py:23
  46.9 15.0 %collective-permute-start.23 = (bf16[4,256,128]{2,1,0:T(8,128)(2,1)S(1)}, bf16[4,256,128]{2,1,0:T(8,128)(2,1)S(1)}, u32[]{:S(2)}, u32[]{:S(2)}) collective-permute-start(bf16[4,256,128]{2,1,0:T(8,128)(2,1)S(1)} %get-tuple-element.52), channel_id=1, source_target_pairs={{0,192},{64,128},{128,64},{192,0},{1,193},{65,129},{129,65},{193,1... | collective-permute-start | bytes 786440 | tf_op jit(solution)/shard_map/ppermute | solution.py:23
  50.9 12.1 %collective-permute-start.13 = (bf16[4,256,128]{2,1,0:T(8,128)(2,1)S(1)}, bf16[4,256,128]{2,1,0:T(8,128)(2,1)S(1)}, u32[]{:S(2)}, u32[]{:S(2)}) collective-permute-start(bf16[4,256,128]{2,1,0:T(8,128)(2,1)S(1)} %get-tuple-element.42), channel_id=1, source_target_pairs={{0,64},{64,0},{128,192},{192,128},{1,65},{65,1},{129,193},{193,129... | collective-permute-start | bytes 786440 | tf_op jit(solution)/shard_map/ppermute | solution.py:23
  51.0 20.0 %collective-permute-start.14 = (bf16[4,256,128]{2,1,0:T(8,128)(2,1)S(1)}, bf16[4,256,128]{2,1,0:T(8,128)(2,1)S(1)}, u32[]{:S(2)}, u32[]{:S(2)}) collective-permute-start(bf16[4,256,128]{2,1,0:T(8,128)(2,1)S(1)} %get-tuple-element.43), channel_id=1, source_target_pairs={{0,128},{64,192},{128,0},{192,64},{1,129},{65,193},{129,1},{193,65... | collective-permute-start | bytes 786440 | tf_op jit(solution)/shard_map/ppermute | solution.py:23
  59.0 16.1 %collective-permute-start.15 = (bf16[4,256,128]{2,1,0:T(8,128)(2,1)S(1)}, bf16[4,256,128]{2,1,0:T(8,128)(2,1)S(1)}, u32[]{:S(2)}, u32[]{:S(2)}) collective-permute-start(bf16[4,256,128]{2,1,0:T(8,128)(2,1)S(1)} %get-tuple-element.44), channel_id=1, source_target_pairs={{0,192},{64,128},{128,64},{192,0},{1,193},{65,129},{129,65},{193,1... | collective-permute-start | bytes 786440 | tf_op jit(solution)/shard_map/ppermute | solution.py:23
  59.7 16.3 %collective-permute-start.7 = (bf16[4,256,128]{2,1,0:T(8,128)(2,1)S(1)}, bf16[4,256,128]{2,1,0:T(8,128)(2,1)S(1)}, u32[]{:S(2)}, u32[]{:S(2)}) collective-permute-start(bf16[4,256,128]{2,1,0:T(8,128)(2,1)S(1)} %get-tuple-element.36), channel_id=1, source_target_pairs={{0,64},{64,0},{128,192},{192,128},{1,65},{65,1},{129,193},{193,129... | collective-permute-start | bytes 786440 | tf_op jit(solution)/shard_map/ppermute | solution.py:23
  61.9 22.5 %collective-permute-start.5 = (bf16[4,256,128]{2,1,0:T(8,128)(2,1)S(1)}, bf16[4,256,128]{2,1,0:T(8,128)(2,1)S(1)}, u32[]{:S(2)}, u32[]{:S(2)}) collective-permute-start(bf16[4,256,128]{2,1,0:T(8,128)(2,1)S(1)} %get-tuple-element.33), channel_id=1, source_target_pairs={{0,192},{64,128},{128,64},{192,0},{1,193},{65,129},{129,65},{193,1... | collective-permute-start | bytes 786440 | tf_op jit(solution)/shard_map/ppermute | solution.py:23
  63.0 21.4 %collective-permute-start.6 = (bf16[4,256,128]{2,1,0:T(8,128)(2,1)S(1)}, bf16[4,256,128]{2,1,0:T(8,128)(2,1)S(1)}, u32[]{:S(2)}, u32[]{:S(2)}) collective-permute-start(bf16[4,256,128]{2,1,0:T(8,128)(2,1)S(1)} %get-tuple-element.34), channel_id=1, source_target_pairs={{0,128},{64,192},{128,0},{192,64},{1,129},{65,193},{129,1},{193,65... | collective-permute-start | bytes 786440 | tf_op jit(solution)/shard_map/ppermute | solution.py:23
